TPU v7x, 32 devices: a whole 2x2x4 slice. The times are simulated.
32 devices in a mesh: groups: 2 (over y), dp: 16 (over z, x, core).
Axes of the slice: x: 2, y: 2, z: 4, core: 2. Of those that a mesh axis runs over, the one named last changes fastest.
Arguments:
- query_acts: bfloat16 [4096, 8192], P(('groups', 'dp')), parts along dimension 0, may hold values from -6 to 6
- cotangent: bfloat16 [4096, 8192], P(('groups', 'dp')), parts along dimension 0, may hold values from -6 to 6
- conv_weight: float32 [4, 4, 8192], replicated, may hold values from -3 to 3
- conv_bias: float32 [4, 8192], replicated, may hold values from -3 to 3
- owner_map: int32 [4], replicated, may hold values from 0 to 15, as said below
- basis_store: float32 [16, 25, 8192], P('dp'), may hold values from -2.5 to 2.5
- lambda_store: float32 [16, 5, 8192], P('dp'), may hold values from 0.1 to 10
- train_grads: bfloat16 [256, 4, 5, 8192], P(('groups', 'dp')), parts along dimension 0, may hold values from -6 to 6
- batch_index: int32 [512], P(('groups', 'dp')), parts along dimension 0, may hold values from 0 to 127, as said below
Outputs:
- adjoint_in: bfloat16 [4096, 8192], P(('groups', 'dp')), parts along dimension 0
- scores: float32 [512], P(('groups', 'dp')), parts along dimension 0
There are 2 independent parts, one for each index of `groups`. A program takes and returns all parts, laid end to end along the dimension named above; an argument that names none is the same for every part. Nothing has to cross between parts.
Inputs may be any that keep to these rules, and one draw needn't show every extreme that they name: `owner_map`: the 4 entries are distinct. `batch_index`: entry n names a row from (n // 16) * 8 to (n // 16) * 8 + 7.
All inputs are finite; a program needn't handle non-finite values.
Results may differ from a plain program's by a relative error of at most 0.015.
Values may be sent and summed in bfloat16 or wider, within the bound.
A program may use at most 128 MiB of HBM per device.

v0:
```python
import functools
import math

import jax
import jax.numpy as jnp
import numpy as np
from jax import lax
from jax.experimental import pallas as pl
from jax.experimental.pallas import tpu as pltpu
from jax.sharding import PartitionSpec as P

LANES = 128
SUB = 8
TAPS = 4
HALO_ROWS = 16
PAIRS = [(j, k) for j in range(5) for k in range(j, 5)]


def layout_plan(rows, layers):
    reach = (TAPS - 1) * layers
    extended = rows + 2 * reach
    fold = -(-extended // SUB)
    padded = -(-(fold * SUB) // 16) * 16
    return reach, fold, padded


def permutations(rows, layers):
    reach, fold, padded = layout_plan(rows, layers)
    columns = rows + 2 * HALO_ROWS
    into = np.zeros((padded, columns), np.float32)
    back = np.zeros((rows, padded), np.float32)
    for j in range(fold):
        for s in range(SUB):
            token = fold * s + j - reach
            row = SUB * j + s
            if 0 <= token < rows:
                into[row, token] = 1.0
                back[token, row] = 1.0
            elif -reach <= token < 0:
                into[row, rows + HALO_ROWS + token] = 1.0
            elif rows <= token < rows + reach:
                into[row, HALO_ROWS + token] = 1.0
    return jnp.asarray(into, jnp.bfloat16), jnp.asarray(back, jnp.bfloat16)


def rounded(value):
    return value.astype(jnp.bfloat16).astype(jnp.float32)


def window_chunk(lanes, rows, layers, is_first, w_ref, b_ref, x_all, c_all, slope_all, g_ref):
    reach, fold, padded = layout_plan(rows, layers)
    sub = lax.broadcasted_iota(jnp.int32, (SUB, LANES), 0)
    edges = {}

    def own(j, low, high):
        tokens = [fold * s + j - reach for s in range(SUB)]
        inside = tuple(low <= t < high for t in tokens)
        if all(inside):
            return None
        if inside not in edges:
            lead = next(i for i, ok in enumerate(inside) if ok)
            tail = max(i for i, ok in enumerate(inside) if ok)
            edges[inside] = (sub >= lead) & (sub <= tail)
        return edges[inside]

    zero = jnp.zeros((SUB, LANES), jnp.float32)

    def keep(value, mask):
        return value if mask is None else jnp.where(mask, value, zero)

    def row(ref, *at):
        return jnp.broadcast_to(ref[at[:-1] + (pl.ds(at[-1], 1), lanes)], (SUB, LANES))

    live = {}

    def begun(j):
        mask = own(j, 0, 1 << 30)
        if mask is None:
            return None
        key = id(mask)
        if key not in live:
            live[key] = mask | jnp.logical_not(is_first)
        return live[key]

    last = TAPS - 1
    for layer in range(layers):
        taps = [row(w_ref, layer, k) * 0.5 for k in range(TAPS)]
        bias = row(b_ref, layer) * 0.5
        base = layer * (fold + last) * SUB
        for i in range(last):
            wrapped = x_all[pl.ds(base + (fold + i) * SUB, SUB), lanes]
            x_all[pl.ds(base + i * SUB, SUB), lanes] = pltpu.roll(wrapped, 1, 0)
        x = [x_all[pl.ds(base + i * SUB, SUB), lanes] for i in range(fold + last)]
        following = base + (fold + last + last) * SUB
        for j in range(fold):
            half = bias
            for k in range(TAPS):
                half = half + taps[k] * x[last + j - k]
            bent = jnp.tanh(half)
            up = 1.0 + bent
            slope_all[pl.ds((layer * fold + j) * SUB, SUB), lanes] = up * (1.0 + half * (1.0 - bent))
            if layer < layers - 1:
                fresh = keep(rounded(x[last + j] + half * up), begun(j))
                x_all[pl.ds(following + j * SUB, SUB), lanes] = fresh
    for layer in reversed(range(layers)):
        taps = [row(w_ref, layer, k) * 0.5 for k in range(TAPS)]
        base = layer * (fold + last) * SUB
        doubled = [None] * (fold + last)
        sums = [zero] * (TAPS + 1)

        def at(i):
            return x_all[pl.ds(base + i * SUB, SUB), lanes]

        for j in range(fold):
            adjoint = c_all[pl.ds(j * SUB, SUB), lanes]
            slope = slope_all[pl.ds((layer * fold + j) * SUB, SUB), lanes]
            grad = keep(rounded(adjoint * slope), own(j, 0, 1 << 30))
            doubled[j] = grad
            if j < last:
                doubled[fold + j] = pltpu.roll(grad, SUB - 1, 0)
            inner = keep(grad, own(j, -(1 << 30), rows))
            for k in range(TAPS):
                sums[k] = sums[k] + at(last + j - k) * inner
            sums[TAPS] = sums[TAPS] + inner
        for j in range(fold):
            total = c_all[pl.ds(j * SUB, SUB), lanes]
            back = taps[0] * doubled[j]
            for k in range(1, TAPS):
                back = back + taps[k] * doubled[j + k]
            c_all[pl.ds(j * SUB, SUB), lanes] = rounded(total + back)
        for k in range(TAPS + 1):
            g_ref[pl.ds(layer * 5 + k, 1), lanes] = 0.5 * jnp.sum(sums[k], axis=0, keepdims=True)


def window_kernel(rows, layers, x_ref, c_ref, hx_ref, hc_ref, w_ref, b_ref, into_ref, back_ref,
                  out_ref, g_ref, x_all, c_all, slope_all):
    reach, fold, padded = layout_plan(rows, layers)
    width = x_ref.shape[1]
    is_first = lax.axis_index("dp") == 0
    count = fold * SUB
    acts = jnp.concatenate([x_ref[...], hx_ref[...]], axis=0)
    cots = jnp.concatenate([c_ref[...], hc_ref[...]], axis=0)
    x_all[pl.ds((TAPS - 1) * SUB, count), :] = jnp.dot(
        into_ref[...], acts, preferred_element_type=jnp.float32)[:count]
    c_all[...] = jnp.dot(into_ref[...], cots, preferred_element_type=jnp.float32)

    @pl.loop(0, width // LANES)
    def _(chunk):
        lanes = pl.ds(pl.multiple_of(chunk * LANES, LANES), LANES)
        window_chunk(lanes, rows, layers, is_first, w_ref, b_ref, x_all, c_all, slope_all, g_ref)

    out_ref[...] = jnp.dot(
        back_ref[...], c_all[...].astype(jnp.bfloat16), preferred_element_type=jnp.float32
    ).astype(jnp.bfloat16)


def window(acts, cots, halo_acts, halo_cots, weights, bias):
    rows, channels = acts.shape
    layers = weights.shape[0]
    reach, fold, padded = layout_plan(rows, layers)
    width = 512
    into, back = permutations(rows, layers)
    block = lambda *lead: pl.BlockSpec(lead + (width,), lambda i: (0,) * len(lead) + (i,))
    whole = lambda a: pl.BlockSpec(a.shape, lambda i: (0, 0))
    return pl.pallas_call(
        functools.partial(window_kernel, rows, layers),
        grid=(channels // width,),
        out_shape=(
            jax.ShapeDtypeStruct((rows, channels), jnp.bfloat16),
            jax.ShapeDtypeStruct((layers * 5, channels), jnp.float32),
        ),
        in_specs=[
            block(rows), block(rows), block(2 * HALO_ROWS), block(2 * HALO_ROWS),
            block(layers, TAPS), block(layers), whole(into), whole(back),
        ],
        out_specs=(block(rows), block(layers * 5)),
        scratch_shapes=[
            pltpu.VMEM((layers * (fold + TAPS - 1) * SUB, width), jnp.float32),
            pltpu.VMEM((padded, width), jnp.float32),
            pltpu.VMEM((layers * fold * SUB, width), jnp.float32),
        ],
        compiler_params=pltpu.CompilerParams(vmem_limit_bytes=24 << 20),
        cost_estimate=pl.CostEstimate(flops=200_000_000, bytes_accessed=10_000_000, transcendentals=5_000_000),
    )(acts, cots, halo_acts, halo_cots, weights, bias, into, back)


def shifted(value, axis, steps):
    count = lax.axis_size(axis)
    first, final = (max(0, -steps), min(count, count - steps))
    return lax.ppermute(value, axis, [(s, s + steps) for s in range(first, final)])


def inverse_rows(basis, vals):
    channels = basis.shape[-1]
    blocks = basis.reshape(5, 5, channels)
    scale = 1.0 / (vals + 0.1 * jnp.mean(vals))
    return jnp.stack([jnp.sum(blocks[j] * blocks[k] * scale, axis=0) for j, k in PAIRS])


def exchange_kernel(count, layers, scale, owner_ref, g_ref, m_ref, p_ref,
                    got_g, got_m, part, full, send_g, recv_g, send_m, recv_m, send_p, recv_p):
    here = lax.axis_index("dp")
    share = part.shape[1]
    mine = pl.ds(pl.multiple_of(here * share, LANES), share)
    barrier = pltpu.get_barrier_semaphore()
    for step in range(1, count):
        pl.semaphore_signal(barrier, inc=1, device_id={"dp": lax.rem(here + step, count)},
                            device_id_type=pl.DeviceIdType.MESH)
    pl.semaphore_wait(barrier, count - 1)
    copies = []
    for step in range(1, count):
        target = lax.rem(here + step, count)
        theirs = pl.ds(pl.multiple_of(target * share, LANES), share)
        for source, slots, sent, got in ((g_ref, got_g, send_g, recv_g), (m_ref, got_m, send_m, recv_m)):
            copy = pltpu.make_async_remote_copy(
                src_ref=source.at[:, theirs], dst_ref=slots.at[step],
                send_sem=sent.at[step], recv_sem=got.at[step],
                device_id={"dp": target}, device_id_type=pl.DeviceIdType.MESH)
            copy.start()
            copies.append(copy)
    got_m[0] = m_ref[:, mine]
    for copy in copies:
        copy.wait()
    total = g_ref[:, mine]
    for step in range(1, count):
        total = total + got_g[step]
    total = total * scale
    order = {pair: i for i, pair in enumerate(PAIRS)}
    for layer in range(layers):
        slot = lax.rem(here - owner_ref[layer] + count, count)
        inverse = got_m[slot].astype(jnp.float32)
        for j in range(5):
            value = None
            for k in range(5):
                i = order[min(j, k), max(j, k)]
                term = inverse[i:i + 1] * total[layer * 5 + k:layer * 5 + k + 1]
                value = term if value is None else value + term
            part[pl.ds(layer * 5 + j, 1), :] = value
    copies = []
    for step in range(1, count):
        copy = pltpu.make_async_remote_copy(
            src_ref=part, dst_ref=full.at[:, mine],
            send_sem=send_p.at[step], recv_sem=recv_p.at[step],
            device_id={"dp": lax.rem(here + step, count)}, device_id_type=pl.DeviceIdType.MESH)
        copy.start()
        copies.append(copy)
    full[:, mine] = part[...]
    for copy in copies:
        copy.wait()
    p_ref[...] = full[...]


def exchanged(partial, rows_sent, owner_map, layers, scale):
    count = lax.axis_size("dp")
    terms, channels = partial.shape
    share = channels // count
    vmem = pl.BlockSpec(memory_space=pltpu.VMEM)
    sems = pltpu.SemaphoreType.DMA((count,))
    return pl.pallas_call(
        functools.partial(exchange_kernel, count, layers, scale),
        out_shape=jax.ShapeDtypeStruct((terms, channels), jnp.float32),
        in_specs=[pl.BlockSpec(memory_space=pltpu.SMEM), vmem, vmem],
        out_specs=vmem,
        scratch_shapes=[
            pltpu.VMEM((count, terms, share), jnp.float32),
            pltpu.VMEM((count, rows_sent.shape[0], share), rows_sent.dtype),
            pltpu.VMEM((terms, share), jnp.float32),
            pltpu.VMEM((terms, channels), jnp.float32),
        ] + [sems] * 6,
        compiler_params=pltpu.CompilerParams(
            collective_id=0, has_side_effects=True, vmem_limit_bytes=24 << 20),
    )(owner_map, partial, rows_sent)


def on_device(query_acts, cotangent, conv_weight, conv_bias, owner_map, basis_store, lambda_store,
              train_grads, batch_index):
    rows, channels = query_acts.shape
    layers = conv_weight.shape[0]
    here = lax.axis_index("dp")
    norm_scale = 1.0 / math.sqrt(rows * lax.axis_size("dp"))
    before = shifted(query_acts[rows - HALO_ROWS:], "dp", 1)
    after = shifted(jnp.concatenate([query_acts[:HALO_ROWS], cotangent[:HALO_ROWS]]), "dp", -1)
    halo_acts = jnp.concatenate([before, after[:HALO_ROWS]])
    halo_cots = jnp.concatenate([jnp.zeros_like(before), after[HALO_ROWS:]])
    own_rows = inverse_rows(basis_store[0], lambda_store[0])
    adjoint, partial = window(query_acts, cotangent, halo_acts, halo_cots, conv_weight, conv_bias)
    if channels % (LANES * lax.axis_size("dp")) == 0:
        sent = jnp.concatenate([own_rows, own_rows[:1]]).astype(jnp.bfloat16)
        everyone = exchanged(partial, sent, owner_map, layers, norm_scale)
        everyone = everyone.reshape(layers, 5, channels)
    else:
        held = jnp.where((owner_map == here)[:, None, None], own_rows[None], 0.0)
        inverse = lax.psum(held, "dp")
        summed = (lax.psum(partial, "dp") * norm_scale).reshape(layers, 5, channels)
        order = {pair: i for i, pair in enumerate(PAIRS)}
        everyone = jnp.stack([
            sum(inverse[:, order[min(j, k), max(j, k)]] * summed[:, k] for k in range(5))
            for j in range(5)
        ], axis=1)
    high = everyone.astype(jnp.bfloat16)
    low = (everyone - high.astype(jnp.float32)).astype(jnp.bfloat16)
    both = high.astype(jnp.float32) + low.astype(jnp.float32)
    examples = train_grads.shape[0]
    values = jnp.sum(train_grads.astype(jnp.float32) * both[None], axis=(1, 2, 3))
    values = values * (1.0 / math.sqrt(5 * layers * channels))
    local_index = batch_index - here * examples
    chosen = local_index[:, None] == jnp.arange(examples, dtype=jnp.int32)[None, :]
    scores = jnp.sum(jnp.where(chosen, values[None, :], 0.0), axis=1)
    return (adjoint, scores)


def solution(mesh):
    in_specs = (
        P(("groups", "dp"), None),
        P(("groups", "dp"), None),
        P(),
        P(),
        P(),
        P("dp", None, None),
        P("dp", None, None),
        P(("groups", "dp"), None, None, None),
        P(("groups", "dp")),
    )
    out_specs = (P(("groups", "dp"), None), P(("groups", "dp")))
    return jax.shard_map(
        on_device, mesh=mesh, in_specs=in_specs, out_specs=out_specs, check_vma=False
    )
```

profile of v0, /device:TPU:11, one launch (start us, length us, event | category | flops | bytes accessed | tf_op | source)
XLA Modules:
  0.0 116.3 jit_solution(18011542379538046152)
XLA Ops:
  0.6 0.0 copy-start.8
  0.6 0.0 copy-start.7
  0.7 1.1 slice.27
  1.7 1.1 fusion.1
  2.8 0.8 pad_maximum_fusion
  3.6 2.6 %collective-permute-start.1 = (bf16[32,8192]{1,0:T(8,128)(2,1)}, bf16[32,8192]{1,0:T(8,128)(2,1)}, u32[]{:S(2)}, u32[]{:S(2)}) collective-permute-start(bf16[32,8192]{1,0:T(8,128)(2,1)} %pad_maximum_fusion), channel_id=1, source_target_pairs={{1,0},{2,1},{3,2},{4,3},{5,4},{6,5},{7,6},{8,7},{9,8},{10,9},{11,1... | collective-permute-start | bytes 1572872 | tf_op jit(solution)/shard_map/ppermute | solution.py:190
  6.2 3.9 %collective-permute-start = (bf16[16,8192]{1,0:T(8,128)(2,1)S(1)}, bf16[16,8192]{1,0:T(8,128)(2,1)}, u32[]{:S(2)}, u32[]{:S(2)}) collective-permute-start(bf16[16,8192]{1,0:T(8,128)(2,1)S(1)} %get-tuple-element.22), channel_id=1, source_target_pairs={{0,1},{1,2},{2,3},{3,4},{4,5},{5,6},{6,7},{7,8},{8,9},{9,10},{10,1... | collective-permute-start | bytes 786440 | tf_op jit(solution)/shard_map/ppermute | solution.py:190
  10.1 0.0 copy-done.8
  10.1 0.9 reduce_sum.162
  11.7 0.0 copy-done.7
  11.7 2.9 %multiply_reduce_fusion.1 = (bf16[8192]{0:T(1024)(128)(2,1)S(1)}, bf16[8192]{0:T(1024)(128)(2,1)S(1)}, bf16[8192]{0:T(1024)(128)(2,1)S(1)}, bf16[8192]{0:T(1024)...) fusion(f32[1,25,8192]{2,0,1:T(1,128)S(1)} %copy-done.7, ...), kind=kLoop, calls=%fused_computation.6 | loop fusion | flops 1343488 | bytes 1327108 | tf_op jit(solution)/shard_map/reduce_sum | solution.py:197
  14.6 0.0 copy-start
  14.6 0.0 copy-start.3
  14.6 0.0 copy-start.4
  14.7 0.0 copy-start.5
  14.7 0.0 copy-start.6
  14.7 2.3 %multiply_reduce_fusion.12 = (bf16[8192]{0:T(1024)(128)(2,1)S(1)}, bf16[8192]{0:T(1024)(128)(2,1)S(1)}, bf16[8192]{0:T(1024)(128)(2,1)S(1)}, bf16[8192]{0:T(1024)(128)(2,1)S(1)}) fusion(f32[1,5,8192]{2,0,1:T(1,128)S(1)} %get-tuple-element.21, f32[1,25,8192]{2,0,1:T(1,128)} %param.16), kind=kLoop, calls=%fused_computation.17 | loop fusion | flops 458752 | bytes 884736 | tf_op jit(solution)/shard_map/reduce_sum | solution.py:197
  17.1 0.6 stack.63
  17.7 0.6 stack.64
  18.3 0.6 stack.65
  18.9 0.6 stack.66
  19.5 0.6 stack.67
  20.2 0.6 stack.68
  20.8 0.6 stack.69
  21.4 0.6 stack.70
  22.0 0.6 stack.71
  22.6 0.6 stack.72
  23.3 0.6 stack.73
  23.9 2.4 %concatenate.16.m_ref = bf16[16,8192]{1,0:T(8,128)(2,1)S(1)} concatenate(bf16[1,8192]{1,0:T(2,128)(2,1)S(1)} %reshape.69, bf16[1,8192]{1,0:T(2,128)(2,1)S(1)} %stack.60, bf16[1,8192]{1,0:T(2,128)(2,1)S(1)} %stack.61, bf16[1,8192]{1,0:T(2,128)(2,1)S(1)} %stack.62, bf16[1,8192]{1,0:T(2,128)(2,1)} %stack.63, bf16[1,8192]{1,0:T(2,128)(2,1)} %stack.64, bf16[1,8192]{1,0:T(2,128)(2,1)} %stack.65, ...), dimensions={0} | concatenate | bytes 524288 | tf_op jit(solution)/shard_map/concatenate | solution.py:288
  26.3 0.0 copy-start.1
  26.3 0.8 broadcast_subtract_fusion
  27.1 0.0 collective-permute-done.1
  27.1 1.1 fusion.2
  28.2 0.0 collective-permute-done
  28.2 1.0 pad_maximum_fusion.1.hx_ref
  29.2 0.0 copy-done
  29.2 0.0 copy-done.3
  29.2 0.0 copy-done.4
  29.3 0.0 copy-done.5
  29.3 0.0 copy-done.6
  29.3 0.0 copy-start.2
  29.3 37.3 %shard_map.122 = (bf16[128,8192]{1,0:T(8,128)(2,1)}, f32[20,8192]{1,0:T(8,128)S(1)}) custom-call(bf16[128,8192]{1,0:T(8,128)(2,1)S(1)} %copy-done, bf16[128,8192]{1,0:T(8,128)(2,1)S(1)} %copy-done.1, bf16[32,8192]{1,0:T(8,128)(2,1)S(1)} %pad_maximum_fusion.1.hx_ref, bf16[32,8192]{1,0:T(8,128)(2,1)S(1)} %concatenate.15.hc_ref, f32[4,4,8192]{2,1,0:T(4,128)S(1)} %copy-done.3, ...), custom_call_target="tpu_custom_call" | custom-call | flops 200000000 | bytes 10000000 | tf_op jit(solution)/shard_map/pallas_call | solution.py:165
  66.6 0.0 copy-done.2
  66.6 45.2 %shard_map.123 = f32[20,8192]{1,0:T(8,128)S(1)} custom-call(s32[4]{0:T(128)S(1)} %copy-done.2, f32[20,8192]{1,0:T(8,128)S(1)} %get-tuple-element.5.g_ref, bf16[16,8192]{1,0:T(8,128)(2,1)S(1)} %concatenate.16.m_ref), custom_call_target="tpu_custom_call" | custom-call | tf_op jit(solution)/shard_map/pallas_call | solution.py:259
  111.9 0.1 reshape.68
  112.0 0.4 convert_add_fusion
  112.4 3.3 %multiply_reduce_fusion = f32[8]{0:T(128)S(1)} fusion(bf16[8,4,5,8192]{3,1,2,0:T(4,128)(2,1)} %param.18, f32[4,5,8192]{2,0,1:T(4,128)S(1)} %convert_add_fusion), kind=kLoop, calls=%fused_computation | loop fusion | flops 3932152 | bytes 3276832 | tf_op jit(solution)/shard_map/reduce_sum | solution.py:304
  115.7 0.6 select_reduce_fusion
  (7 shorter events, 0.1 us)
Async XLA Ops:
  0.6 9.4 %copy-start.8 = (f32[1,5,8192]{2,0,1:T(1,128)S(1)}, f32[1,5,8192]{2,0,1:T(1,128)}, u32[]{:S(2)}) copy-start(f32[1,5,8192]{2,0,1:T(1,128)} %param.17) | copy-start | bytes 491524
  0.6 11.0 %copy-start.7 = (f32[1,25,8192]{2,0,1:T(1,128)S(1)}, f32[1,25,8192]{2,0,1:T(1,128)}, u32[]{:S(2)}) copy-start(f32[1,25,8192]{2,0,1:T(1,128)} %param.16) | copy-start | bytes 2457604
  3.6 23.5 %collective-permute-start.1 = (bf16[32,8192]{1,0:T(8,128)(2,1)}, bf16[32,8192]{1,0:T(8,128)(2,1)}, u32[]{:S(2)}, u32[]{:S(2)}) collective-permute-start(bf16[32,8192]{1,0:T(8,128)(2,1)} %pad_maximum_fusion), channel_id=1, source_target_pairs={{1,0},{2,1},{3,2},{4,3},{5,4},{6,5},{7,6},{8,7},{9,8},{10,9},{11,1... | collective-permute-start | bytes 1572872 | tf_op jit(solution)/shard_map/ppermute | solution.py:190
  6.2 22.0 %collective-permute-start = (bf16[16,8192]{1,0:T(8,128)(2,1)S(1)}, bf16[16,8192]{1,0:T(8,128)(2,1)}, u32[]{:S(2)}, u32[]{:S(2)}) collective-permute-start(bf16[16,8192]{1,0:T(8,128)(2,1)S(1)} %get-tuple-element.22), channel_id=1, source_target_pairs={{0,1},{1,2},{2,3},{3,4},{4,5},{5,6},{6,7},{7,8},{8,9},{9,10},{10,1... | collective-permute-start | bytes 786440 | tf_op jit(solution)/shard_map/ppermute | solution.py:190
  14.6 14.6 %copy-start = (bf16[128,8192]{1,0:T(8,128)(2,1)S(1)}, bf16[128,8192]{1,0:T(8,128)(2,1)}, u32[]{:S(2)}) copy-start(bf16[128,8192]{1,0:T(8,128)(2,1)} %x_ref.1) | copy-start | bytes 6291460
  14.6 14.6 %copy-start.3 = (f32[4,4,8192]{2,1,0:T(4,128)S(1)}, f32[4,4,8192]{2,1,0:T(4,128)}, u32[]{:S(2)}) copy-start(f32[4,4,8192]{2,1,0:T(4,128)} %w_ref.1) | copy-start | bytes 1572868
  14.6 14.6 %copy-start.4 = (f32[4,8192]{1,0:T(4,128)S(1)}, f32[4,8192]{1,0:T(4,128)}, u32[]{:S(2)}) copy-start(f32[4,8192]{1,0:T(4,128)} %b_ref.1) | copy-start | bytes 393220
  14.7 14.6 %copy-start.5 = (bf16[160,160]{1,0:T(8,128)(2,1)S(1)}, bf16[160,160]{1,0:T(8,128)(2,1)}, u32[]{:S(2)}) copy-start(bf16[160,160]{1,0:T(8,128)(2,1)} %constant.23.clone.into_ref) | copy-start | bytes 153604
  14.7 14.6 %copy-start.6 = (bf16[128,160]{1,0:T(8,128)(2,1)S(1)}, bf16[128,160]{1,0:T(8,128)(2,1)}, u32[]{:S(2)}) copy-start(bf16[128,160]{1,0:T(8,128)(2,1)} %constant.24.clone.back_ref) | copy-start | bytes 122884
  26.3 3.0 %copy-start.1 = (bf16[128,8192]{1,0:T(8,128)(2,1)S(1)}, bf16[128,8192]{1,0:T(8,128)(2,1)}, u32[]{:S(2)}) copy-start(bf16[128,8192]{1,0:T(8,128)(2,1)} %c_ref.1) | copy-start | bytes 6291460
  29.3 37.3 %copy-start.2 = (s32[4]{0:T(128)S(1)}, s32[4]{0:T(128)}, u32[]{:S(2)}) copy-start(s32[4]{0:T(128)} %owner_ref.1) | copy-start | bytes 52
where the time goes:
time: 117 us; the launch traced here: 116 us
  Pallas kernels  82.6 us (71%)
  other arithmetic  13 us (11%)
  local copies, waits for them, and re-layouts  12.7 us (11%)
  starting transfers between devices  6.45 us (6%)
  between operations  1.54 us (1%)
    pallas_call x1, Pallas kernels, exchanged(): pl.pallas_call(functools.partial(exchange_kernel, count, layers, scale),...  45.2 us
    pallas_call x1, Pallas kernels, window(): pl.pallas_call(functools.partial(window_kernel, rows, layers), grid=(chan...  37.3 us
    another operation x14, local copies, waits for them, and re-layouts, inverse_rows(): jnp.stack([jnp.sum(blocks[j] * blocks[k] * scale, axis=0) for j, k in PAI...  6.9 us
    ppermute x2, starting transfers between devices, shifted(): lax.ppermute(value, axis, [(s, s + steps) for s in range(first, final)])  6.45 us
    reduce_sum x2, other arithmetic, inverse_rows(): jnp.sum(blocks[j] * blocks[k] * scale, axis=0)  5.18 us
    reduce_sum x1, other arithmetic, on_device(): jnp.sum(train_grads.astype(jnp.float32) * both[None], axis=(1, 2, 3))  3.26 us
    concatenate x1, local copies, waits for them, and re-layouts, on_device(): sent = jnp.concatenate([own_rows, own_rows[:1]]).astype(jnp.bfloat16)  2.39 us
  transfers between devices with their start and end apart: 2, of which 0 were waited for; matrix products, arithmetic and copies ran while one was open for 15% of the time, Pallas kernels for 0%

commit v1 on v0

--- a/solution.py
+++ b/solution.py
@@ -197,33 +197,285 @@
     return jnp.stack([jnp.sum(blocks[j] * blocks[k] * scale, axis=0) for j, k in PAIRS])
 
 
-def exchange_kernel(count, layers, scale, owner_ref, g_ref, m_ref, p_ref,
-                    got_g, got_m, part, full, send_g, recv_g, send_m, recv_m, send_p, recv_p):
+ROWS8 = 8
+HALO = 16
+
+
+def token_permutation(invert):
+    row = lax.broadcasted_iota(jnp.int32, (LANES, LANES), 0)
+    col = lax.broadcasted_iota(jnp.int32, (LANES, LANES), 1)
+    if invert:
+        row, col = col, row
+    same = ((row >> 3) == (col & 15)) & ((row & 7) == (col >> 4))
+    return jnp.where(same, 1.0, 0.0).astype(jnp.bfloat16)
+
+
+def forward_layer(layer, layers, rows, step, tile, x_all, s_all, w_all, keep):
+    taps = [w_all[layer * TAPS + k, tile, :] * 0.5 for k in range(TAPS)]
+    bias = w_all[layers * TAPS + layer, tile, :] * 0.5
+
+    def span(first, n, mask=None):
+        x = [x_all[layer, first - 3 + i] for i in range(n + 3)]
+        for i in range(n):
+            half = ((taps[0] * x[i + 3] + taps[1] * x[i + 2]) + (taps[2] * x[i + 1] + taps[3] * x[i])) + bias
+            bent = jnp.tanh(half)
+            up = 1.0 + bent
+            s_all[layer, first + i] = up * (1.0 + half * (1.0 - bent))
+            if layer < layers - 1:
+                fresh = x[i + 3] + half * up
+                x_all[layer + 1, first + i] = fresh if mask is None else fresh * mask
+
+    early = 3 * (layers - 1 - layer)
+    if early:
+        span(HALO - early, early, keep)
+    total = rows + 3 * layers
+    full, rest = total // step, total % step
+
+    @pl.loop(0, full)
+    def _(j):
+        span(HALO + j * step, step)
+
+    if rest:
+        span(HALO + full * step, rest)
+
+
+def pairwise(values):
+    while len(values) > 1:
+        values = [values[i] + values[i + 1] if i + 1 < len(values) else values[i]
+                  for i in range(0, len(values), 2)]
+    return values[0]
+
+
+def backward_layer(layer, layers, rows, step, tile, x_all, s_all, a_all, w_all, g_all):
+    taps = [w_all[layer * TAPS + k, tile, :] * 0.5 for k in range(TAPS)]
+
+    def grads(first, n):
+        return [a_all[first + i] * s_all[layer, HALO + first + i] for i in range(n)]
+
+    def back(first, dv, n):
+        for i in range(n):
+            a_all[first + i] = a_all[first + i] + (
+                (taps[0] * dv[i] + taps[1] * dv[i + 1]) + (taps[2] * dv[i + 2] + taps[3] * dv[i + 3]))
+
+    def sums(first, dv, n):
+        x = [x_all[layer, HALO + first - 3 + i] for i in range(n + 3)]
+        terms = [pairwise([x[i + 3 - k] * dv[i] for i in range(n)]) for k in range(TAPS)]
+        return terms + [pairwise(dv[:n])]
+
+    def body(j, carry):
+        first = j * step
+        dv = list(carry[:3]) + grads(first + 3, step)
+        part = sums(first, dv, step)
+        back(first, dv, step)
+        return tuple(dv[step:step + 3]) + tuple(a + b for a, b in zip(carry[3:], part))
+
+    zero = jnp.zeros((ROWS8, LANES), jnp.float32)
+    carry = lax.fori_loop(0, rows // step, body, tuple(grads(0, 3)) + (zero,) * (TAPS + 1))
+    for k in range(TAPS + 1):
+        g_all[layer * 5 + k] = 0.5 * carry[3 + k]
+    extra = 3 * layer
+    if extra:
+        dv = list(carry[:3]) + grads(rows + 3, extra)
+        back(rows, dv, extra)
+
+
+def fused_kernel(count, layers, rows, channels, scale, owner_ref, x_hbm, c_hbm, w_hbm, b_hbm, q_hbm, l_hbm,
+                 out_hbm, p_ref, xh, ch, wv, bv, qv, lv, w_all, x_all, s_all, a_all, g_all, ov,
+                 ms, got_m, gs, got_g, part, full_p,
+                 load, store, send_h, recv_h, send_m, recv_m, send_g, recv_g, send_p, recv_p):
     here = lax.axis_index("dp")
-    share = part.shape[1]
-    mine = pl.ds(pl.multiple_of(here * share, LANES), share)
+    width = ROWS8 * LANES
+    groups = channels // width
+    share = channels // count
+    lines = share // LANES
+    per = ROWS8 // lines
+
+    def remote(source, target_ref, sent, got, device):
+        return pltpu.make_async_remote_copy(
+            src_ref=source, dst_ref=target_ref, send_sem=sent, recv_sem=got,
+            device_id={"dp": device}, device_id_type=pl.DeviceIdType.MESH)
+
+    locals_ = [
+        pltpu.make_async_copy(q_hbm, qv, load.at[0]),
+        pltpu.make_async_copy(l_hbm, lv, load.at[1]),
+        pltpu.make_async_copy(w_hbm, wv, load.at[2]),
+        pltpu.make_async_copy(b_hbm, bv, load.at[3]),
+        pltpu.make_async_copy(x_hbm, xh.at[pl.ds(HALO, rows), :], load.at[4]),
+        pltpu.make_async_copy(c_hbm, ch.at[pl.ds(0, rows), :], load.at[5]),
+    ]
+    for copy in locals_:
+        copy.start()
     barrier = pltpu.get_barrier_semaphore()
-    for step in range(1, count):
+
+    @pl.loop(1, count)
+    def _(step):
         pl.semaphore_signal(barrier, inc=1, device_id={"dp": lax.rem(here + step, count)},
                             device_id_type=pl.DeviceIdType.MESH)
+
     pl.semaphore_wait(barrier, count - 1)
-    copies = []
+
+    def lanes_of(group):
+        return pl.ds(pl.multiple_of(group * width, width), width)
+
+    def group_at(device, i):
+        return lax.rem(lax.div(device, per) + 1 + i, groups)
+
+    def halo(kind, group, device):
+        lanes = lanes_of(group)
+        if kind == 0:
+            source, target = x_hbm.at[pl.ds(rows - HALO, HALO), lanes], xh.at[pl.ds(0, HALO), lanes]
+        elif kind == 1:
+            source, target = x_hbm.at[pl.ds(0, HALO), lanes], xh.at[pl.ds(rows + HALO, HALO), lanes]
+        else:
+            source, target = c_hbm.at[pl.ds(0, HALO), lanes], ch.at[pl.ds(rows, HALO), lanes]
+        return remote(source, target, send_h.at[kind, group], recv_h.at[kind, group], device)
+
+    @pl.loop(0, groups)
+    def _(i):
+        @pl.when(here < count - 1)
+        def _():
+            halo(0, group_at(here + 1, i), here + 1).start()
+
+        @pl.when(here > 0)
+        def _():
+            group = group_at(here - 1, i)
+            halo(1, group, here - 1).start()
+            halo(2, group, here - 1).start()
+
+    @pl.when(here == 0)
+    def _():
+        xh[pl.ds(0, HALO), :] = jnp.zeros((HALO, channels), jnp.bfloat16)
+
+    @pl.when(here == count - 1)
+    def _():
+        xh[pl.ds(rows + HALO, HALO), :] = jnp.zeros((HALO, channels), jnp.bfloat16)
+        ch[pl.ds(rows, HALO), :] = jnp.zeros((HALO, channels), jnp.bfloat16)
+
+    locals_[0].wait()
+    locals_[1].wait()
+    damping = 0.1 * jnp.mean(lv[...])
+
+    @pl.loop(0, groups)
+    def _(o):
+        tile = pl.ds(pl.multiple_of(o * ROWS8, ROWS8), ROWS8)
+        inverse = [1.0 / (lv[i, tile, :] + damping) for i in range(5)]
+        basis = [[qv[j * 5 + i, tile, :] for i in range(5)] for j in range(5)]
+        for at, (j, k) in enumerate(PAIRS):
+            value = basis[j][0] * basis[k][0] * inverse[0]
+            for i in range(1, 5):
+                value = value + basis[j][i] * basis[k][i] * inverse[i]
+            for h in range(per):
+                ms[o * per + h, at] = value[h * lines:(h + 1) * lines].astype(jnp.bfloat16)
+
+    def send_rows(step):
+        target = lax.rem(here + step, count)
+        return remote(ms.at[target], got_m.at[step], send_m.at[step], recv_m.at[step], target)
+
+    @pl.loop(1, count)
+    def _(step):
+        send_rows(step).start()
+
+    got_m[0] = ms[here]
+    locals_[2].wait()
+    locals_[3].wait()
+
+    @pl.loop(0, channels // LANES)
+    def _(g):
+        lanes = pl.ds(pl.multiple_of(g * LANES, LANES), LANES)
+        for layer in range(layers):
+            for k in range(TAPS):
+                w_all[layer * TAPS + k, pl.ds(g, 1), :] = wv[layer, pl.ds(k, 1), lanes]
+            w_all[layers * TAPS + layer, pl.ds(g, 1), :] = bv[pl.ds(layer, 1), lanes]
+
+    into, back = token_permutation(False), token_permutation(True)
+    keep = jnp.where(here > 0, 1.0, 0.0) * jnp.ones((ROWS8, LANES), jnp.float32)
+    locals_[4].wait()
+    locals_[5].wait()
+
+    def gather_block(ref, at, base):
+        return jnp.concatenate(
+            [ref[pl.ds(at, HALO), pl.ds(pl.multiple_of(base + g * LANES, LANES), LANES)] for g in range(ROWS8)],
+            axis=0)
+
+    def give(group, h):
+        owner = group * per + h
+        return remote(gs.at[owner], got_g.at[here], send_g.at[owner], recv_g.at[here], owner)
+
+    def written(group):
+        return pltpu.make_async_copy(ov.at[:, lanes_of(group)], out_hbm.at[:, lanes_of(group)], store.at[group])
+
+    @pl.loop(0, groups)
+    def _(turn):
+        group = group_at(here, turn)
+        base = group * width
+        tile = pl.ds(pl.multiple_of(group * ROWS8, ROWS8), ROWS8)
+
+        @pl.when(here > 0)
+        def _():
+            halo(0, group, here - 1).wait_recv()
+
+        @pl.when(here < count - 1)
+        def _():
+            halo(1, group, here + 1).wait_recv()
+            halo(2, group, here + 1).wait_recv()
+
+        def arrange(source, target, at):
+            pair = jnp.concatenate([gather_block(source, at, base), gather_block(source, at + HALO, base)], axis=1)
+            moved = jnp.dot(into, pair, preferred_element_type=jnp.float32)
+            target[pl.ds(at, HALO)] = moved[:, :LANES].reshape(HALO, ROWS8, LANES)
+            target[pl.ds(at + HALO, HALO)] = moved[:, LANES:].reshape(HALO, ROWS8, LANES)
+
+        @pl.loop(0, (rows + 2 * HALO) // (2 * HALO))
+        def _(b):
+            arrange(xh, x_all.at[0], pl.multiple_of(b * 2 * HALO, 2 * HALO))
+
+        @pl.loop(0, rows // (2 * HALO))
+        def _(b):
+            arrange(ch, a_all, pl.multiple_of(b * 2 * HALO, 2 * HALO))
+
+        moved = jnp.dot(into, gather_block(ch, rows, base), preferred_element_type=jnp.float32)
+        a_all[pl.ds(rows, HALO)] = moved.reshape(HALO, ROWS8, LANES)
+
+        for layer in range(layers):
+            forward_layer(layer, layers, rows, 8, tile, x_all, s_all, w_all, keep)
+        for layer in reversed(range(layers)):
+            backward_layer(layer, layers, rows, 8, tile, x_all, s_all, a_all, w_all, g_all)
+
+        for h in range(per):
+            for term in range(layers * 5):
+                gs[group * per + h, term] = g_all[term, h * lines:(h + 1) * lines].astype(jnp.bfloat16)
+
+        for h in range(per):
+            @pl.when(group * per + h != here)
+            def _():
+                give(group, h).start()
+
+        @pl.loop(0, rows // (2 * HALO))
+        def _(b):
+            at = pl.multiple_of(b * 2 * HALO, 2 * HALO)
+            pair = jnp.concatenate(
+                [a_all[pl.ds(at, HALO)].reshape(LANES, LANES), a_all[pl.ds(at + HALO, HALO)].reshape(LANES, LANES)],
+                axis=1).astype(jnp.bfloat16)
+            moved = jnp.dot(back, pair, preferred_element_type=jnp.float32).astype(jnp.bfloat16)
+            for g in range(ROWS8):
+                lanes = pl.ds(pl.multiple_of(base + g * LANES, LANES), LANES)
+                ov[pl.ds(at, HALO), lanes] = moved[g * HALO:(g + 1) * HALO, :LANES]
+                ov[pl.ds(at + HALO, HALO), lanes] = moved[g * HALO:(g + 1) * HALO, LANES:]
+
+        written(group).start()
+
+    @pl.loop(1, count)
+    def _(step):
+        send_rows(step).wait()
+
+    @pl.loop(1, count)
+    def _(step):
+        source = lax.rem(here + step, count)
+        remote(gs.at[source], got_g.at[source], send_g.at[source], recv_g.at[source], source).wait()
+
+    total = gs[here].astype(jnp.float32)
     for step in range(1, count):
-        target = lax.rem(here + step, count)
-        theirs = pl.ds(pl.multiple_of(target * share, LANES), share)
-        for source, slots, sent, got in ((g_ref, got_g, send_g, recv_g), (m_ref, got_m, send_m, recv_m)):
-            copy = pltpu.make_async_remote_copy(
-                src_ref=source.at[:, theirs], dst_ref=slots.at[step],
-                send_sem=sent.at[step], recv_sem=got.at[step],
-                device_id={"dp": target}, device_id_type=pl.DeviceIdType.MESH)
-            copy.start()
-            copies.append(copy)
-    got_m[0] = m_ref[:, mine]
-    for copy in copies:
-        copy.wait()
-    total = g_ref[:, mine]
-    for step in range(1, count):
-        total = total + got_g[step]
+        total = total + got_g[lax.rem(here + step, count)].astype(jnp.float32)
     total = total * scale
     order = {pair: i for i, pair in enumerate(PAIRS)}
     for layer in range(layers):
@@ -232,71 +484,128 @@
         for j in range(5):
             value = None
             for k in range(5):
-                i = order[min(j, k), max(j, k)]
-                term = inverse[i:i + 1] * total[layer * 5 + k:layer * 5 + k + 1]
+                term = inverse[order[min(j, k), max(j, k)]] * total[layer * 5 + k]
                 value = term if value is None else value + term
-            part[pl.ds(layer * 5 + j, 1), :] = value
-    copies = []
-    for step in range(1, count):
-        copy = pltpu.make_async_remote_copy(
-            src_ref=part, dst_ref=full.at[:, mine],
-            send_sem=send_p.at[step], recv_sem=recv_p.at[step],
-            device_id={"dp": lax.rem(here + step, count)}, device_id_type=pl.DeviceIdType.MESH)
-        copy.start()
-        copies.append(copy)
-    full[:, mine] = part[...]
-    for copy in copies:
-        copy.wait()
-    p_ref[...] = full[...]
-
-
-def exchanged(partial, rows_sent, owner_map, layers, scale):
+            for r in range(lines):
+                part[j, pl.ds(layer, 1), r * LANES:(r + 1) * LANES] = value[r:r + 1]
+
+    mine = pl.ds(pl.multiple_of(here * share, share), share)
+
+    def send_part(step):
+        return remote(part, full_p.at[:, :, mine], send_p.at[step], recv_p.at[step], lax.rem(here + step, count))
+
+    @pl.loop(1, count)
+    def _(step):
+        send_part(step).start()
+
+    full_p[:, :, mine] = part[...]
+
+    @pl.loop(0, groups)
+    def _(i):
+        written(i).wait()
+
+        @pl.when(here < count - 1)
+        def _():
+            halo(0, i, here + 1).wait_send()
+
+        @pl.when(here > 0)
+        def _():
+            halo(1, i, here - 1).wait_send()
+            halo(2, i, here - 1).wait_send()
+
+    @pl.loop(1, count)
+    def _(step):
+        send_part(step).wait()
+
+    p_ref[...] = full_p[...]
+
+
+def fused(acts, cots, weights, bias, owner_map, basis, vals, scale):
+    rows, channels = acts.shape
+    layers = weights.shape[0]
     count = lax.axis_size("dp")
-    terms, channels = partial.shape
     share = channels // count
+    lines = share // LANES
+    groups = channels // (ROWS8 * LANES)
+    held = rows + 2 * HALO
     vmem = pl.BlockSpec(memory_space=pltpu.VMEM)
-    sems = pltpu.SemaphoreType.DMA((count,))
+    anywhere = pl.BlockSpec(memory_space=pl.ANY)
+    dma = pltpu.SemaphoreType.DMA
+    f32, b16 = jnp.float32, jnp.bfloat16
+    tall = channels // LANES
     return pl.pallas_call(
-        functools.partial(exchange_kernel, count, layers, scale),
-        out_shape=jax.ShapeDtypeStruct((terms, channels), jnp.float32),
-        in_specs=[pl.BlockSpec(memory_space=pltpu.SMEM), vmem, vmem],
-        out_specs=vmem,
+        functools.partial(fused_kernel, count, layers, rows, channels, scale),
+        out_shape=(
+            jax.ShapeDtypeStruct((rows, channels), b16),
+            jax.ShapeDtypeStruct((5, layers, channels), f32),
+        ),
+        in_specs=[pl.BlockSpec(memory_space=pltpu.SMEM)] + [anywhere] * 6,
+        out_specs=(anywhere, vmem),
         scratch_shapes=[
-            pltpu.VMEM((count, terms, share), jnp.float32),
-            pltpu.VMEM((count, rows_sent.shape[0], share), rows_sent.dtype),
-            pltpu.VMEM((terms, share), jnp.float32),
-            pltpu.VMEM((terms, channels), jnp.float32),
-        ] + [sems] * 6,
+            pltpu.VMEM((held, channels), b16),
+            pltpu.VMEM((rows + HALO, channels), b16),
+            pltpu.VMEM(weights.shape, f32),
+            pltpu.VMEM(bias.shape, f32),
+            pltpu.VMEM((25, tall, LANES), f32),
+            pltpu.VMEM((5, tall, LANES), f32),
+            pltpu.VMEM((layers * 5, tall, LANES), f32),
+            pltpu.VMEM((layers, held, ROWS8, LANES), f32),
+            pltpu.VMEM((layers, held, ROWS8, LANES), f32),
+            pltpu.VMEM((rows + HALO, ROWS8, LANES), f32),
+            pltpu.VMEM((layers * 5, ROWS8, LANES), f32),
+            pltpu.VMEM((rows, channels), b16),
+            pltpu.VMEM((count, len(PAIRS), lines, LANES), b16),
+            pltpu.VMEM((count, len(PAIRS), lines, LANES), b16),
+            pltpu.VMEM((count, layers * 5, lines, LANES), b16),
+            pltpu.VMEM((count, layers * 5, lines, LANES), b16),
+            pltpu.VMEM((5, layers, share), f32),
+            pltpu.VMEM((5, layers, channels), f32),
+            dma((6,)), dma((groups,)),
+            dma((3, groups)), dma((3, groups)),
+            dma((count,)), dma((count,)), dma((count,)), dma((count,)), dma((count,)), dma((count,)),
+        ],
         compiler_params=pltpu.CompilerParams(
-            collective_id=0, has_side_effects=True, vmem_limit_bytes=24 << 20),
-    )(owner_map, partial, rows_sent)
-
-
-def on_device(query_acts, cotangent, conv_weight, conv_bias, owner_map, basis_store, lambda_store,
-              train_grads, batch_index):
+            collective_id=0, has_side_effects=True, vmem_limit_bytes=48 << 20),
+    )(owner_map, acts, cots, weights, bias, basis.reshape(25, tall, LANES), vals.reshape(5, tall, LANES))
+
+
+def precondition_apart(query_acts, cotangent, conv_weight, conv_bias, owner_map, basis_store, lambda_store,
+                       norm_scale):
     rows, channels = query_acts.shape
     layers = conv_weight.shape[0]
     here = lax.axis_index("dp")
-    norm_scale = 1.0 / math.sqrt(rows * lax.axis_size("dp"))
     before = shifted(query_acts[rows - HALO_ROWS:], "dp", 1)
     after = shifted(jnp.concatenate([query_acts[:HALO_ROWS], cotangent[:HALO_ROWS]]), "dp", -1)
     halo_acts = jnp.concatenate([before, after[:HALO_ROWS]])
     halo_cots = jnp.concatenate([jnp.zeros_like(before), after[HALO_ROWS:]])
     own_rows = inverse_rows(basis_store[0], lambda_store[0])
     adjoint, partial = window(query_acts, cotangent, halo_acts, halo_cots, conv_weight, conv_bias)
-    if channels % (LANES * lax.axis_size("dp")) == 0:
-        sent = jnp.concatenate([own_rows, own_rows[:1]]).astype(jnp.bfloat16)
-        everyone = exchanged(partial, sent, owner_map, layers, norm_scale)
-        everyone = everyone.reshape(layers, 5, channels)
+    held = jnp.where((owner_map == here)[:, None, None], own_rows[None], 0.0)
+    inverse = lax.psum(held, "dp")
+    summed = (lax.psum(partial, "dp") * norm_scale).reshape(layers, 5, channels)
+    order = {pair: i for i, pair in enumerate(PAIRS)}
+    everyone = jnp.stack([
+        sum(inverse[:, order[min(j, k), max(j, k)]] * summed[:, k] for k in range(5))
+        for j in range(5)
+    ], axis=1)
+    return adjoint, everyone
+
+
+def on_device(query_acts, cotangent, conv_weight, conv_bias, owner_map, basis_store, lambda_store,
+              train_grads, batch_index):
+    rows, channels = query_acts.shape
+    layers = conv_weight.shape[0]
+    count = lax.axis_size("dp")
+    here = lax.axis_index("dp")
+    norm_scale = 1.0 / math.sqrt(rows * count)
+    lines = channels // (LANES * count)
+    if lines in (4, 8) and channels == lines * LANES * count and rows % (2 * HALO) == 0:
+        adjoint, everyone = fused(query_acts, cotangent, conv_weight, conv_bias, owner_map, basis_store[0],
+                                  lambda_store[0], norm_scale)
+        everyone = everyone.transpose(1, 0, 2)
     else:
-        held = jnp.where((owner_map == here)[:, None, None], own_rows[None], 0.0)
-        inverse = lax.psum(held, "dp")
-        summed = (lax.psum(partial, "dp") * norm_scale).reshape(layers, 5, channels)
-        order = {pair: i for i, pair in enumerate(PAIRS)}
-        everyone = jnp.stack([
-            sum(inverse[:, order[min(j, k), max(j, k)]] * summed[:, k] for k in range(5))
-            for j in range(5)
-        ], axis=1)
+        adjoint, everyone = precondition_apart(query_acts, cotangent, conv_weight, conv_bias, owner_map,
+                                               basis_store, lambda_store, norm_scale)
     high = everyone.astype(jnp.bfloat16)
     low = (everyone - high.astype(jnp.float32)).astype(jnp.bfloat16)
     both = high.astype(jnp.float32) + low.astype(jnp.float32)

time: 117 us -> 84.5 us (0.72)
  other arithmetic: 13 us -> 2.24 us
  Pallas kernels: 82.6 us -> 74.5 us
  local copies, waits for them, and re-layouts: 12.7 us -> 5.98 us
  starting transfers between devices: 6.45 us -> 0 us
    pallas_call x2 -> x1, Pallas kernels: 82.6 us -> 74.5 us  [fused(): pl.pallas_call(functools.partial(fused_kernel, count, layers, rows, chann...]
    another operation x15 -> x0, local copies, waits for them, and re-layouts: 6.92 us -> none  [the longest x14 6.9 us: inverse_rows(): jnp.stack([jnp.sum(blocks[j] * blocks[k] * scale, axis=0) for j, k in PAI...]
    ppermute x2 -> x0, starting transfers between devices: 6.45 us -> none  [shifted(): lax.ppermute(value, axis, [(s, s + steps) for s in range(first, final)])]
    reduce_sum x3 -> x0, other arithmetic: 6.12 us -> none  [the longest x2 5.18 us: inverse_rows(): jnp.sum(blocks[j] * blocks[k] * scale, axis=0)]
    unnamed x18 -> x15, local copies, waits for them, and re-layouts: 0.06 us -> 5.98 us
    slice x3 -> x0, local copies, waits for them, and re-layouts: 3.18 us -> none  [the longest x1 1.07 us: on_device(): before = shifted(query_acts[rows - HALO_ROWS:], 'dp', 1)]
    concatenate x2 -> x0, local copies, waits for them, and re-layouts: 2.43 us -> none  [the longest x1 2.39 us: on_device(): sent = jnp.concatenate([own_rows, own_rows[:1]]).astype(jnp.bfloat16)]
    concatenate x2 -> x0, other arithmetic: 1.81 us -> none  [the longest x1 0.99 us: on_device(): halo_acts = jnp.concatenate([before, after[:HALO_ROWS]])]
  transfers between devices with their start and end apart: 2 -> 0, of which waited for: 0 -> 0; matrix products, arithmetic and copies ran while one was open for 15% -> 0% of each run, Pallas kernels for 0% -> 0%
where the time goes in v1:
time: 84.5 us; the launch traced here: 83.4 us
  Pallas kernels  74.5 us (88%)
  local copies, waits for them, and re-layouts  5.98 us (7%)
  other arithmetic  2.24 us (3%)
    pallas_call x1, Pallas kernels, fused(): pl.pallas_call(functools.partial(fused_kernel, count, layers, rows, chann...  74.5 us
    unnamed x15, local copies, waits for them, and re-layouts  5.98 us

profile of v1, /device:TPU:11, one launch (start us, length us, event | category | flops | bytes accessed | tf_op | source)
XLA Modules:
  0.0 83.4 jit_solution(6847585146970155060)
XLA Ops:
  0.6 0.0 copy-start
  0.6 1.1 %copy-done = f32[1,25,8192]{2,0,1:T(1,128)S(1)} copy-done((f32[1,25,8192]{2,0,1:T(1,128)S(1)}, f32[1,25,8192]{2,0,1:T(1,128)}, u32[]{:S(2)}) %copy-start) | copy-done | bytes 819224
  1.8 0.0 copy-start.1
  1.8 1.0 %copy-done.1 = f32[4,4,8192]{2,1,0:T(4,128)S(1)} copy-done((f32[4,4,8192]{2,1,0:T(4,128)S(1)}, f32[4,4,8192]{2,1,0:T(4,128)}, u32[]{:S(2)}) %copy-start.1) | copy-done | bytes 524312
  2.8 0.0 copy-start.2
  2.8 0.9 %copy-done.2 = f32[1,5,8192]{2,0,1:T(1,128)S(1)} copy-done((f32[1,5,8192]{2,0,1:T(1,128)S(1)}, f32[1,5,8192]{2,0,1:T(1,128)}, u32[]{:S(2)}) %copy-start.2) | copy-done | bytes 163864
  3.7 0.0 copy-start.3
  3.7 0.9 %copy-done.3 = f32[4,8192]{1,0:T(4,128)S(1)} copy-done((f32[4,8192]{1,0:T(4,128)S(1)}, f32[4,8192]{1,0:T(4,128)}, u32[]{:S(2)}) %copy-start.3) | copy-done | bytes 131096
  4.6 0.0 copy-start.4
  4.6 0.7 copy-done.4
  5.3 0.0 copy-start.5
  5.3 74.5 %shard_map.104 = (bf16[128,8192]{1,0:T(8,128)(2,1)S(1)}, f32[5,4,8192]{2,1,0:T(4,128)S(1)}) custom-call(s32[4]{0:T(128)S(1)} %copy-done.4, bf16[128,8192]{1,0:T(8,128)(2,1)} %x_hbm.1, bf16[128,8192]{1,0:T(8,128)(2,1)} %c_hbm.1, f32[4,4,8192]{2,1,0:T(4,128)S(1)} %copy-done.1, f32[4,8192]{1,0:T(4,128)S(1)} %copy-done.3, f32[25,64,128]{2,1,0:T(8,128)S(1)} %bitcast.11, ...), custom_call_target="tpu_custom_call" | custom-call | tf_op jit(solution)/shard_map/pallas_call | solution.py:536
  79.8 0.0 copy-start.6
  79.8 0.1 convert_add_fusion
  80.0 0.0 copy-done.5
  80.0 1.5 %multiply_reduce_fusion = f32[8]{0:T(128)S(1)} fusion(bf16[8,4,5,8192]{3,1,2,0:T(4,128)(2,1)S(1)} %copy-done.5, f32[4,5,8192]{2,0,1:T(4,128)S(1)} %convert_add_fusion), kind=kLoop, calls=%fused_computation | loop fusion | flops 3932152 | bytes 3276832 | tf_op jit(solution)/shard_map/reduce_sum | solution.py:613
  81.5 0.0 copy-done.6
  81.5 0.6 select_reduce_fusion
  82.1 1.3 %copy.12 = bf16[128,8192]{1,0:T(8,128)(2,1)} copy(bf16[128,8192]{1,0:T(8,128)(2,1)S(1)} %get-tuple-element.8) | data formatting | bytes 4194304
  (2 shorter events, 0.0 us)
Async XLA Ops:
  0.6 1.1 %copy-start = (f32[1,25,8192]{2,0,1:T(1,128)S(1)}, f32[1,25,8192]{2,0,1:T(1,128)}, u32[]{:S(2)}) copy-start(f32[1,25,8192]{2,0,1:T(1,128)} %param.14) | copy-start | bytes 2457604
  1.8 1.0 %copy-start.1 = (f32[4,4,8192]{2,1,0:T(4,128)S(1)}, f32[4,4,8192]{2,1,0:T(4,128)}, u32[]{:S(2)}) copy-start(f32[4,4,8192]{2,1,0:T(4,128)} %w_hbm.1) | copy-start | bytes 1572868
  2.8 0.9 %copy-start.2 = (f32[1,5,8192]{2,0,1:T(1,128)S(1)}, f32[1,5,8192]{2,0,1:T(1,128)}, u32[]{:S(2)}) copy-start(f32[1,5,8192]{2,0,1:T(1,128)} %param.15) | copy-start | bytes 491524
  3.7 0.9 %copy-start.3 = (f32[4,8192]{1,0:T(4,128)S(1)}, f32[4,8192]{1,0:T(4,128)}, u32[]{:S(2)}) copy-start(f32[4,8192]{1,0:T(4,128)} %b_hbm.1) | copy-start | bytes 393220
  4.6 0.7 copy-start.4
  5.3 74.7 %copy-start.5 = (bf16[8,4,5,8192]{3,1,2,0:T(4,128)(2,1)S(1)}, bf16[8,4,5,8192]{3,1,2,0:T(4,128)(2,1)}, u32[]{:S(2)}) copy-start(bf16[8,4,5,8192]{3,1,2,0:T(4,128)(2,1)} %param.16) | copy-start | bytes 7864324
  79.8 1.7 %copy-start.6 = (s32[16]{0:T(128)S(1)}, s32[16]{0:T(128)}, u32[]{:S(2)}) copy-start(s32[16]{0:T(128)} %param.17) | copy-start | bytes 196

commit v2 on v1

--- a/solution.py
+++ b/solution.py
@@ -279,9 +279,9 @@
         back(rows, dv, extra)
 
 
-def fused_kernel(count, layers, rows, channels, scale, owner_ref, x_hbm, c_hbm, w_hbm, b_hbm, q_hbm, l_hbm,
+def fused_kernel(count, layers, rows, channels, scale, final, o_hbm, x_hbm, c_hbm, w_hbm, b_hbm, q_hbm, l_hbm, t_hbm,
                  out_hbm, p_ref, xh, ch, wv, bv, qv, lv, w_all, x_all, s_all, a_all, g_all, ov,
-                 ms, got_m, gs, got_g, part, full_p,
+                 ms, got_m, gs, got_g, part, full_p, tv, sacc, owner_ref,
                  load, store, send_h, recv_h, send_m, recv_m, send_g, recv_g, send_p, recv_p):
     here = lax.axis_index("dp")
     width = ROWS8 * LANES
@@ -302,6 +302,8 @@
         pltpu.make_async_copy(b_hbm, bv, load.at[3]),
         pltpu.make_async_copy(x_hbm, xh.at[pl.ds(HALO, rows), :], load.at[4]),
         pltpu.make_async_copy(c_hbm, ch.at[pl.ds(0, rows), :], load.at[5]),
+        pltpu.make_async_copy(o_hbm, owner_ref, load.at[6]),
+        pltpu.make_async_copy(t_hbm, tv, load.at[7]),
     ]
     for copy in locals_:
         copy.start()
@@ -371,10 +373,6 @@
         target = lax.rem(here + step, count)
         return remote(ms.at[target], got_m.at[step], send_m.at[step], recv_m.at[step], target)
 
-    @pl.loop(1, count)
-    def _(step):
-        send_rows(step).start()
-
     got_m[0] = ms[here]
     locals_[2].wait()
     locals_[3].wait()
@@ -419,22 +417,14 @@
             halo(1, group, here + 1).wait_recv()
             halo(2, group, here + 1).wait_recv()
 
-        def arrange(source, target, at):
-            pair = jnp.concatenate([gather_block(source, at, base), gather_block(source, at + HALO, base)], axis=1)
-            moved = jnp.dot(into, pair, preferred_element_type=jnp.float32)
-            target[pl.ds(at, HALO)] = moved[:, :LANES].reshape(HALO, ROWS8, LANES)
-            target[pl.ds(at + HALO, HALO)] = moved[:, LANES:].reshape(HALO, ROWS8, LANES)
-
-        @pl.loop(0, (rows + 2 * HALO) // (2 * HALO))
-        def _(b):
-            arrange(xh, x_all.at[0], pl.multiple_of(b * 2 * HALO, 2 * HALO))
-
-        @pl.loop(0, rows // (2 * HALO))
-        def _(b):
-            arrange(ch, a_all, pl.multiple_of(b * 2 * HALO, 2 * HALO))
-
-        moved = jnp.dot(into, gather_block(ch, rows, base), preferred_element_type=jnp.float32)
-        a_all[pl.ds(rows, HALO)] = moved.reshape(HALO, ROWS8, LANES)
+        def arrange(source, target, blocks):
+            wide = jnp.concatenate([gather_block(source, b * HALO, base) for b in range(blocks)], axis=1)
+            moved = jnp.dot(into, wide, preferred_element_type=jnp.float32)
+            for b in range(blocks):
+                target[pl.ds(b * HALO, HALO)] = moved[:, b * LANES:(b + 1) * LANES].reshape(HALO, ROWS8, LANES)
+
+        arrange(xh, x_all.at[0], rows // HALO + 2)
+        arrange(ch, a_all, rows // HALO + 1)
 
         for layer in range(layers):
             forward_layer(layer, layers, rows, 8, tile, x_all, s_all, w_all, keep)
@@ -450,19 +440,22 @@
             def _():
                 give(group, h).start()
 
-        @pl.loop(0, rows // (2 * HALO))
-        def _(b):
-            at = pl.multiple_of(b * 2 * HALO, 2 * HALO)
-            pair = jnp.concatenate(
-                [a_all[pl.ds(at, HALO)].reshape(LANES, LANES), a_all[pl.ds(at + HALO, HALO)].reshape(LANES, LANES)],
-                axis=1).astype(jnp.bfloat16)
-            moved = jnp.dot(back, pair, preferred_element_type=jnp.float32).astype(jnp.bfloat16)
+        wide = jnp.concatenate(
+            [a_all[pl.ds(b * HALO, HALO)].reshape(LANES, LANES).astype(jnp.bfloat16) for b in range(rows // HALO)],
+            axis=1)
+        moved = jnp.dot(back, wide, preferred_element_type=jnp.float32).astype(jnp.bfloat16)
+        for b in range(rows // HALO):
             for g in range(ROWS8):
                 lanes = pl.ds(pl.multiple_of(base + g * LANES, LANES), LANES)
-                ov[pl.ds(at, HALO), lanes] = moved[g * HALO:(g + 1) * HALO, :LANES]
-                ov[pl.ds(at + HALO, HALO), lanes] = moved[g * HALO:(g + 1) * HALO, LANES:]
+                ov[pl.ds(b * HALO, HALO), lanes] = moved[g * HALO:(g + 1) * HALO, b * LANES:(b + 1) * LANES]
 
         written(group).start()
+
+        @pl.when(turn == 0)
+        def _():
+            @pl.loop(1, count)
+            def _(step):
+                send_rows(step).start()
 
     @pl.loop(1, count)
     def _(step):
@@ -473,6 +466,7 @@
         source = lax.rem(here + step, count)
         remote(gs.at[source], got_g.at[source], send_g.at[source], recv_g.at[source], source).wait()
 
+    locals_[6].wait()
     total = gs[here].astype(jnp.float32)
     for step in range(1, count):
         total = total + got_g[lax.rem(here + step, count)].astype(jnp.float32)
@@ -489,16 +483,72 @@
             for r in range(lines):
                 part[j, pl.ds(layer, 1), r * LANES:(r + 1) * LANES] = value[r:r + 1]
 
-    mine = pl.ds(pl.multiple_of(here * share, share), share)
-
-    def send_part(step):
-        return remote(part, full_p.at[:, :, mine], send_p.at[step], recv_p.at[step], lax.rem(here + step, count))
-
-    @pl.loop(1, count)
-    def _(step):
-        send_part(step).start()
-
-    full_p[:, :, mine] = part[...]
+    core, side, depth = lax.rem(here, 2), lax.rem(lax.div(here, 2), 2), count // 4
+    mate = here + 1 - 2 * core
+    across = here + 2 - 4 * side
+
+    def along(device, i):
+        return lax.rem(device + 4 * i, count)
+
+    def span_of(owner):
+        return pl.ds(pl.multiple_of(owner * share, share), share)
+
+    def pass_on(owner, target, slot):
+        lanes = span_of(owner)
+        return remote(full_p.at[:, :, lanes], full_p.at[:, :, lanes], send_p.at[slot], recv_p.at[owner], target)
+
+    def score(owner):
+        lanes = span_of(owner)
+        both = []
+        for j in range(5):
+            value = full_p[j, :, lanes]
+            high = value.astype(jnp.bfloat16).astype(jnp.float32)
+            both.append(high + (value - high).astype(jnp.bfloat16).astype(jnp.float32))
+        for e in range(tv.shape[0]):
+            value = tv[e, 0, :, lanes].astype(jnp.float32) * both[0]
+            for j in range(1, 5):
+                value = value + tv[e, j, :, lanes].astype(jnp.float32) * both[j]
+            sacc[e] = sacc[e] + value
+
+    full_p[:, :, span_of(here)] = part[...]
+    sends = []
+
+    def send(owner, target):
+        copy = pass_on(owner, target, len(sends))
+        copy.start()
+        sends.append(copy)
+
+    def await_part(owner):
+        pass_on(owner, mate, 0).wait_recv()
+
+    for i in range(1, depth):
+        send(here, along(here, i))
+    send(here, across)
+    send(here, mate)
+    sacc[...] = jnp.zeros_like(sacc)
+    locals_[7].wait()
+    score(here)
+    for i in range(1, depth):
+        await_part(along(here, i))
+        send(along(here, i), across)
+        send(along(here, i), mate)
+    await_part(across)
+    send(across, mate)
+    for i in range(1, depth):
+        score(along(here, i))
+    for i in range(1, depth):
+        await_part(along(across, i))
+        send(along(across, i), mate)
+    for i in range(depth):
+        score(along(across, i))
+    for owner in (mate, mate + 2 - 4 * side):
+        for i in range(depth):
+            await_part(along(owner, i))
+            score(along(owner, i))
+
+    for e in range(tv.shape[0]):
+        rowed = jnp.sum(jnp.sum(sacc[e], axis=0, keepdims=True), axis=1, keepdims=True)
+        p_ref[pl.ds(e, 1), :] = jnp.broadcast_to(rowed * final, (1, LANES))
 
     @pl.loop(0, groups)
     def _(i):
@@ -513,14 +563,11 @@
             halo(1, i, here - 1).wait_send()
             halo(2, i, here - 1).wait_send()
 
-    @pl.loop(1, count)
-    def _(step):
-        send_part(step).wait()
-
-    p_ref[...] = full_p[...]
-
-
-def fused(acts, cots, weights, bias, owner_map, basis, vals, scale):
+    for copy in sends:
+        copy.wait_send()
+
+
+def fused(acts, cots, weights, bias, owner_map, basis, vals, train, scale, final):
     rows, channels = acts.shape
     layers = weights.shape[0]
     count = lax.axis_size("dp")
@@ -529,17 +576,17 @@
     groups = channels // (ROWS8 * LANES)
     held = rows + 2 * HALO
     vmem = pl.BlockSpec(memory_space=pltpu.VMEM)
-    anywhere = pl.BlockSpec(memory_space=pl.ANY)
+    anywhere = pl.BlockSpec(memory_space=pltpu.HBM)
     dma = pltpu.SemaphoreType.DMA
     f32, b16 = jnp.float32, jnp.bfloat16
     tall = channels // LANES
     return pl.pallas_call(
-        functools.partial(fused_kernel, count, layers, rows, channels, scale),
+        functools.partial(fused_kernel, count, layers, rows, channels, scale, final),
         out_shape=(
             jax.ShapeDtypeStruct((rows, channels), b16),
-            jax.ShapeDtypeStruct((5, layers, channels), f32),
+            jax.ShapeDtypeStruct((train.shape[0], LANES), f32),
         ),
-        in_specs=[pl.BlockSpec(memory_space=pltpu.SMEM)] + [anywhere] * 6,
+        in_specs=[anywhere] * 8,
         out_specs=(anywhere, vmem),
         scratch_shapes=[
             pltpu.VMEM((held, channels), b16),
@@ -560,13 +607,16 @@
             pltpu.VMEM((count, layers * 5, lines, LANES), b16),
             pltpu.VMEM((5, layers, share), f32),
             pltpu.VMEM((5, layers, channels), f32),
-            dma((6,)), dma((groups,)),
+            pltpu.VMEM(train.shape, b16),
+            pltpu.VMEM((train.shape[0], layers, share), f32),
+            pltpu.SMEM(owner_map.shape, owner_map.dtype),
+            dma((8,)), dma((groups,)),
             dma((3, groups)), dma((3, groups)),
             dma((count,)), dma((count,)), dma((count,)), dma((count,)), dma((count,)), dma((count,)),
         ],
         compiler_params=pltpu.CompilerParams(
-            collective_id=0, has_side_effects=True, vmem_limit_bytes=48 << 20),
-    )(owner_map, acts, cots, weights, bias, basis.reshape(25, tall, LANES), vals.reshape(5, tall, LANES))
+            collective_id=0, has_side_effects=True, vmem_limit_bytes=63 << 20),
+    )(owner_map, acts, cots, weights, bias, basis.reshape(25, tall, LANES), vals.reshape(5, tall, LANES), train)
 
 
 def precondition_apart(query_acts, cotangent, conv_weight, conv_bias, owner_map, basis_store, lambda_store,
@@ -599,19 +649,19 @@
     here = lax.axis_index("dp")
     norm_scale = 1.0 / math.sqrt(rows * count)
     lines = channels // (LANES * count)
-    if lines in (4, 8) and channels == lines * LANES * count and rows % (2 * HALO) == 0:
-        adjoint, everyone = fused(query_acts, cotangent, conv_weight, conv_bias, owner_map, basis_store[0],
-                                  lambda_store[0], norm_scale)
-        everyone = everyone.transpose(1, 0, 2)
+    examples = train_grads.shape[0]
+    final = 1.0 / math.sqrt(5 * layers * channels)
+    if lines in (4, 8) and count % 4 == 0 and channels == lines * LANES * count and rows % HALO == 0:
+        adjoint, values = fused(query_acts, cotangent, conv_weight, conv_bias, owner_map, basis_store[0],
+                                lambda_store[0], train_grads.transpose(0, 2, 1, 3), norm_scale, final)
+        values = values[:, 0]
     else:
         adjoint, everyone = precondition_apart(query_acts, cotangent, conv_weight, conv_bias, owner_map,
                                                basis_store, lambda_store, norm_scale)
-    high = everyone.astype(jnp.bfloat16)
-    low = (everyone - high.astype(jnp.float32)).astype(jnp.bfloat16)
-    both = high.astype(jnp.float32) + low.astype(jnp.float32)
-    examples = train_grads.shape[0]
-    values = jnp.sum(train_grads.astype(jnp.float32) * both[None], axis=(1, 2, 3))
-    values = values * (1.0 / math.sqrt(5 * layers * channels))
+        high = everyone.astype(jnp.bfloat16)
+        low = (everyone - high.astype(jnp.float32)).astype(jnp.bfloat16)
+        both = high.astype(jnp.float32) + low.astype(jnp.float32)
+        values = jnp.sum(train_grads.astype(jnp.float32) * both[None], axis=(1, 2, 3)) * final
     local_index = batch_index - here * examples
     chosen = local_index[:, None] == jnp.arange(examples, dtype=jnp.int32)[None, :]
     scores = jnp.sum(jnp.where(chosen, values[None, :], 0.0), axis=1)

time: 84.5 us -> 61.6 us (0.73); the launches traced: 83.4 us -> 61.4 us
  Pallas kernels: 74.5 us -> 56.2 us
  local copies, waits for them, and re-layouts: 5.98 us -> 3.9 us
  other arithmetic: 2.24 us -> 0.6 us
    pallas_call x1, Pallas kernels: 74.5 us -> 56.2 us  [fused(): pl.pallas_call(functools.partial(fused_kernel, count, layers, rows, chann...]
    unnamed x15 -> x3, local copies, waits for them, and re-layouts: 5.98 us -> 3.1 us
    reduce_sum x1 -> x0, other arithmetic: 1.52 us -> none  [on_device(): jnp.sum(train_grads.astype(jnp.float32) * both[None], axis=(1, 2, 3))]
where the time goes in v2:
time: 61.6 us; the launch traced here: 61.4 us
  Pallas kernels  56.2 us (91%)
  local copies, waits for them, and re-layouts  3.9 us (6%)
  between operations  0.66 us (1%)
    pallas_call x1, Pallas kernels, fused(): pl.pallas_call(functools.partial(fused_kernel, count, layers, rows, chann...  56.2 us
    unnamed x3, local copies, waits for them, and re-layouts  3.1 us

profile of v2, /device:TPU:11, one launch (start us, length us, event | category | flops | bytes accessed | tf_op | source)
XLA Modules:
  0.0 61.4 jit_solution(8809834039238082382)
XLA Ops:
  0.6 0.0 copy-start
  0.6 56.2 %shard_map.104 = (bf16[128,8192]{1,0:T(8,128)(2,1)}, f32[8,128]{1,0:T(8,128)}) custom-call(s32[4]{0:T(128)} %o_hbm.1, bf16[128,8192]{1,0:T(8,128)(2,1)} %x_hbm.1, bf16[128,8192]{1,0:T(8,128)(2,1)} %c_hbm.1, f32[4,4,8192]{2,1,0:T(4,128)} %w_hbm.1, f32[4,8192]{1,0:T(4,128)} %b_hbm.1, f32[25,64,128]{2,1,0:T(8,128)} %bitcast.4, f32[5,64,128]{2,1,0:T(8,128)} %bitcast.5, ...), custom_call_target="tpu_custom_call" | custom-call | tf_op jit(solution)/shard_map/pallas_call | solution.py:583
  56.9 0.8 %slice_reduce_fusion = f32[8]{0:T(128)S(1)} fusion(f32[8,128]{1,0:T(8,128)} %get-tuple-element.5), kind=kLoop, calls=%fused_computation.1 | loop fusion | bytes 64 | tf_op jit(solution)/shard_map/slice | solution.py:657
  57.7 0.0 copy-done
  57.7 0.6 select_reduce_fusion
  58.3 3.1 %copy.12 = bf16[128,8192]{1,0:T(8,128)(2,1)} copy(bf16[128,8192]{1,0:T(8,128)(2,1)} %get-tuple-element.8) | data formatting | bytes 4194304
  (1 shorter events, 0.0 us)
Async XLA Ops:
  0.6 57.0 %copy-start = (s32[16]{0:T(128)S(1)}, s32[16]{0:T(128)}, u32[]{:S(2)}) copy-start(s32[16]{0:T(128)} %param.17) | copy-start | bytes 196

commit v3 on v2

--- a/solution.py
+++ b/solution.py
@@ -220,9 +220,10 @@
             half = ((taps[0] * x[i + 3] + taps[1] * x[i + 2]) + (taps[2] * x[i + 1] + taps[3] * x[i])) + bias
             bent = jnp.tanh(half)
             up = 1.0 + bent
-            s_all[layer, first + i] = up * (1.0 + half * (1.0 - bent))
+            gain = half * up
+            s_all[layer, first + i] = up + gain * (1.0 - bent)
             if layer < layers - 1:
-                fresh = x[i + 3] + half * up
+                fresh = x[i + 3] + gain
                 x_all[layer + 1, first + i] = fresh if mask is None else fresh * mask
 
     early = 3 * (layers - 1 - layer)
@@ -332,17 +333,20 @@
             source, target = c_hbm.at[pl.ds(0, HALO), lanes], ch.at[pl.ds(rows, HALO), lanes]
         return remote(source, target, send_h.at[kind, group], recv_h.at[kind, group], device)
 
-    @pl.loop(0, groups)
-    def _(i):
+    def send_halos(turn):
         @pl.when(here < count - 1)
         def _():
-            halo(0, group_at(here + 1, i), here + 1).start()
+            halo(0, group_at(here + 1, turn), here + 1).start()
 
         @pl.when(here > 0)
         def _():
-            group = group_at(here - 1, i)
+            group = group_at(here - 1, turn)
             halo(1, group, here - 1).start()
             halo(2, group, here - 1).start()
+
+    ahead = 2
+    for turn in range(ahead):
+        send_halos(turn)
 
     @pl.when(here == 0)
     def _():
@@ -385,7 +389,7 @@
                 w_all[layer * TAPS + k, pl.ds(g, 1), :] = wv[layer, pl.ds(k, 1), lanes]
             w_all[layers * TAPS + layer, pl.ds(g, 1), :] = bv[pl.ds(layer, 1), lanes]
 
-    into, back = token_permutation(False), token_permutation(True)
+    into = token_permutation(False)
     keep = jnp.where(here > 0, 1.0, 0.0) * jnp.ones((ROWS8, LANES), jnp.float32)
     locals_[4].wait()
     locals_[5].wait()
@@ -400,7 +404,7 @@
         return remote(gs.at[owner], got_g.at[here], send_g.at[owner], recv_g.at[here], owner)
 
     def written(group):
-        return pltpu.make_async_copy(ov.at[:, lanes_of(group)], out_hbm.at[:, lanes_of(group)], store.at[group])
+        return pltpu.make_async_copy(ov.at[group], out_hbm.at[group], store.at[group])
 
     @pl.loop(0, groups)
     def _(turn):
@@ -408,6 +412,10 @@
         base = group * width
         tile = pl.ds(pl.multiple_of(group * ROWS8, ROWS8), ROWS8)
 
+        @pl.when(turn < groups - ahead)
+        def _():
+            send_halos(turn + ahead)
+
         @pl.when(here > 0)
         def _():
             halo(0, group, here - 1).wait_recv()
@@ -440,15 +448,7 @@
             def _():
                 give(group, h).start()
 
-        wide = jnp.concatenate(
-            [a_all[pl.ds(b * HALO, HALO)].reshape(LANES, LANES).astype(jnp.bfloat16) for b in range(rows // HALO)],
-            axis=1)
-        moved = jnp.dot(back, wide, preferred_element_type=jnp.float32).astype(jnp.bfloat16)
-        for b in range(rows // HALO):
-            for g in range(ROWS8):
-                lanes = pl.ds(pl.multiple_of(base + g * LANES, LANES), LANES)
-                ov[pl.ds(b * HALO, HALO), lanes] = moved[g * HALO:(g + 1) * HALO, b * LANES:(b + 1) * LANES]
-
+        ov[group] = a_all[pl.ds(0, rows)].reshape(rows * ROWS8, LANES).astype(jnp.bfloat16)
         written(group).start()
 
         @pl.when(turn == 0)
@@ -583,7 +583,7 @@
     return pl.pallas_call(
         functools.partial(fused_kernel, count, layers, rows, channels, scale, final),
         out_shape=(
-            jax.ShapeDtypeStruct((rows, channels), b16),
+            jax.ShapeDtypeStruct((groups, rows * ROWS8, LANES), b16),
             jax.ShapeDtypeStruct((train.shape[0], LANES), f32),
         ),
         in_specs=[anywhere] * 8,
@@ -600,7 +600,7 @@
             pltpu.VMEM((layers, held, ROWS8, LANES), f32),
             pltpu.VMEM((rows + HALO, ROWS8, LANES), f32),
             pltpu.VMEM((layers * 5, ROWS8, LANES), f32),
-            pltpu.VMEM((rows, channels), b16),
+            pltpu.VMEM((groups, rows * ROWS8, LANES), b16),
             pltpu.VMEM((count, len(PAIRS), lines, LANES), b16),
             pltpu.VMEM((count, len(PAIRS), lines, LANES), b16),
             pltpu.VMEM((count, layers * 5, lines, LANES), b16),
@@ -617,6 +617,75 @@
         compiler_params=pltpu.CompilerParams(
             collective_id=0, has_side_effects=True, vmem_limit_bytes=63 << 20),
     )(owner_map, acts, cots, weights, bias, basis.reshape(25, tall, LANES), vals.reshape(5, tall, LANES), train)
+
+
+def finish_kernel(rows, a_hbm, v_hbm, i_hbm, out_hbm, s_hbm, av, ov, v_ref, i_ref, s_ref, load, store):
+    back = token_permutation(True)
+    blocks = rows // HALO
+    groups = a_hbm.shape[0]
+    width = ROWS8 * LANES
+
+    def read(i):
+        return pltpu.make_async_copy(a_hbm.at[i], av.at[i], load.at[i])
+
+    def write(i):
+        lanes = pl.ds(i * width, width)
+        return pltpu.make_async_copy(ov.at[:, lanes], out_hbm.at[:, lanes], store.at[i])
+
+    for i in range(groups):
+        read(i).start()
+    small = [pltpu.make_async_copy(v_hbm, v_ref, load.at[groups]),
+             pltpu.make_async_copy(i_hbm, i_ref, load.at[groups + 1])]
+    picked = pltpu.make_async_copy(s_ref, s_hbm, store.at[groups])
+    for copy in small:
+        copy.start()
+    examples = v_ref.shape[0]
+    picks = i_ref.shape[1]
+    for i in range(groups):
+        read(i).wait()
+        wide = jnp.concatenate([av[i, pl.ds(b * LANES, LANES), :] for b in range(blocks)], axis=1)
+        moved = jnp.dot(back, wide, preferred_element_type=jnp.float32).astype(jnp.bfloat16)
+        for b in range(blocks):
+            for g in range(ROWS8):
+                ov[pl.ds(b * HALO, HALO), pl.ds(i * width + g * LANES, LANES)] = (
+                    moved[g * HALO:(g + 1) * HALO, b * LANES:(b + 1) * LANES])
+        write(i).start()
+        if i == 0:
+            for copy in small:
+                copy.wait()
+            local = i_ref[...] - lax.axis_index("dp") * examples
+            chosen = jnp.broadcast_to(local, (examples, picks)) == lax.broadcasted_iota(jnp.int32, (examples, picks), 0)
+            s_ref[...] = jnp.sum(jnp.where(chosen, v_ref[:, :picks], 0.0), axis=0, keepdims=True)
+            picked.start()
+    for i in range(groups):
+        write(i).wait()
+    picked.wait()
+
+
+def finish(moved, values, batch_index, rows):
+    groups = moved.shape[0]
+    picks = batch_index.shape[0]
+    channels = groups * ROWS8 * LANES
+    anywhere = pl.BlockSpec(memory_space=pltpu.HBM)
+    return pl.pallas_call(
+        functools.partial(finish_kernel, rows),
+        out_shape=(
+            jax.ShapeDtypeStruct((rows, channels), jnp.bfloat16),
+            jax.ShapeDtypeStruct((1, picks), jnp.float32),
+        ),
+        in_specs=[anywhere] * 3,
+        out_specs=(anywhere, anywhere),
+        scratch_shapes=[
+            pltpu.VMEM(moved.shape, moved.dtype),
+            pltpu.VMEM((rows, channels), moved.dtype),
+            pltpu.VMEM(values.shape, values.dtype),
+            pltpu.VMEM((1, picks), batch_index.dtype),
+            pltpu.VMEM((1, picks), jnp.float32),
+            pltpu.SemaphoreType.DMA((groups + 2,)),
+            pltpu.SemaphoreType.DMA((groups + 1,)),
+        ],
+        compiler_params=pltpu.CompilerParams(vmem_limit_bytes=63 << 20),
+    )(moved, values, batch_index.reshape(1, picks))
 
 
 def precondition_apart(query_acts, cotangent, conv_weight, conv_bias, owner_map, basis_store, lambda_store,
@@ -651,10 +720,12 @@
     lines = channels // (LANES * count)
     examples = train_grads.shape[0]
     final = 1.0 / math.sqrt(5 * layers * channels)
-    if lines in (4, 8) and count % 4 == 0 and channels == lines * LANES * count and rows % HALO == 0:
-        adjoint, values = fused(query_acts, cotangent, conv_weight, conv_bias, owner_map, basis_store[0],
+    if lines in (4, 8) and count % 4 == 0 and channels == lines * LANES * count and (
+            rows % HALO == 0 and batch_index.shape[0] <= LANES):
+        moved, values = fused(query_acts, cotangent, conv_weight, conv_bias, owner_map, basis_store[0],
                                 lambda_store[0], train_grads.transpose(0, 2, 1, 3), norm_scale, final)
-        values = values[:, 0]
+        adjoint, scores = finish(moved, values, batch_index, rows)
+        return (adjoint, scores.reshape(-1))
     else:
         adjoint, everyone = precondition_apart(query_acts, cotangent, conv_weight, conv_bias, owner_map,
                                                basis_store, lambda_store, norm_scale)

time: 61.6 us -> 57.5 us (0.933)
  local copies, waits for them, and re-layouts: 3.9 us -> 0 us
    pallas_call x0 -> x1, Pallas kernels: none -> 3.73 us  [finish(): pl.pallas_call(functools.partial(finish_kernel, rows), out_shape=(jax.Sha...]
    pallas_call x1, Pallas kernels: 56.2 us -> 52.6 us  [fused(): pl.pallas_call(functools.partial(fused_kernel, count, layers, rows, chann...]
    unnamed x3 -> x0, local copies, waits for them, and re-layouts: 3.1 us -> none
    slice x1 -> x0, local copies, waits for them, and re-layouts: 0.8 us -> none  [on_device(): values = values[:, 0]]
where the time goes in v3:
time: 57.5 us; the launch traced here: 57 us
  Pallas kernels  56.3 us (98%)
  between operations  0.64 us (1%)
    pallas_call x1, Pallas kernels, fused(): pl.pallas_call(functools.partial(fused_kernel, count, layers, rows, chann...  52.6 us
    pallas_call x1, Pallas kernels, finish(): pl.pallas_call(functools.partial(finish_kernel, rows), out_shape=(jax.Sha...  3.73 us

profile of v3, /device:TPU:11, one launch (start us, length us, event | category | flops | bytes accessed | tf_op | source)
XLA Modules:
  0.0 57.0 jit_solution(4407654324374918318)
XLA Ops:
  0.6 52.6 %shard_map.104 = (bf16[8,1024,128]{2,1,0:T(8,128)(2,1)}, f32[8,128]{1,0:T(8,128)}) custom-call(s32[4]{0:T(128)} %o_hbm.1, bf16[128,8192]{1,0:T(8,128)(2,1)} %x_hbm.1, bf16[128,8192]{1,0:T(8,128)(2,1)} %c_hbm.1, f32[4,4,8192]{2,1,0:T(4,128)} %w_hbm.1, f32[4,8192]{1,0:T(4,128)} %b_hbm.1, f32[25,64,128]{2,1,0:T(8,128)} %bitcast.6, f32[5,64,128]{2,1,0:T(8,128)} %bitcast.7, ...), custom_call_target="tpu_custom_call" | custom-call | tf_op jit(solution)/shard_map/pallas_call | solution.py:583
  53.2 3.7 %shard_map.105 = (bf16[128,8192]{1,0:T(8,128)(2,1)}, f32[1,16]{1,0:T(1,128)}) custom-call(bf16[8,1024,128]{2,1,0:T(8,128)(2,1)} %get-tuple-element.6.a_hbm, f32[8,128]{1,0:T(8,128)} %get-tuple-element.7.v_hbm, s32[1,16]{1,0:T(1,128)} %bitcast.8), custom_call_target="tpu_custom_call" | custom-call | tf_op jit(solution)/shard_map/pallas_call | solution.py:670

commit v4 on v3

--- a/solution.py
+++ b/solution.py
@@ -281,7 +281,7 @@
 
 
 def fused_kernel(count, layers, rows, channels, scale, final, o_hbm, x_hbm, c_hbm, w_hbm, b_hbm, q_hbm, l_hbm, t_hbm,
-                 out_hbm, p_ref, xh, ch, wv, bv, qv, lv, w_all, x_all, s_all, a_all, g_all, ov,
+                 out_hbm, p_ref, xh, ch, wv, bv, qv, lv, w_all, x_all, s_all, a_all, g_all, ov, ot,
                  ms, got_m, gs, got_g, part, full_p, tv, sacc, owner_ref,
                  load, store, send_h, recv_h, send_m, recv_m, send_g, recv_g, send_p, recv_p):
     here = lax.axis_index("dp")
@@ -389,7 +389,7 @@
                 w_all[layer * TAPS + k, pl.ds(g, 1), :] = wv[layer, pl.ds(k, 1), lanes]
             w_all[layers * TAPS + layer, pl.ds(g, 1), :] = bv[pl.ds(layer, 1), lanes]
 
-    into = token_permutation(False)
+    into, back = token_permutation(False), token_permutation(True)
     keep = jnp.where(here > 0, 1.0, 0.0) * jnp.ones((ROWS8, LANES), jnp.float32)
     locals_[4].wait()
     locals_[5].wait()
@@ -404,7 +404,7 @@
         return remote(gs.at[owner], got_g.at[here], send_g.at[owner], recv_g.at[here], owner)
 
     def written(group):
-        return pltpu.make_async_copy(ov.at[group], out_hbm.at[group], store.at[group])
+        return pltpu.make_async_copy(ot.at[:, lanes_of(group)], out_hbm.at[:, lanes_of(group)], store.at[group])
 
     @pl.loop(0, groups)
     def _(turn):
@@ -435,9 +435,9 @@
         arrange(ch, a_all, rows // HALO + 1)
 
         for layer in range(layers):
-            forward_layer(layer, layers, rows, 8, tile, x_all, s_all, w_all, keep)
+            forward_layer(layer, layers, rows, (rows + 3 * layers) // 2, tile, x_all, s_all, w_all, keep)
         for layer in reversed(range(layers)):
-            backward_layer(layer, layers, rows, 8, tile, x_all, s_all, a_all, w_all, g_all)
+            backward_layer(layer, layers, rows, 16, tile, x_all, s_all, a_all, w_all, g_all)
 
         for h in range(per):
             for term in range(layers * 5):
@@ -449,8 +449,6 @@
                 give(group, h).start()
 
         ov[group] = a_all[pl.ds(0, rows)].reshape(rows * ROWS8, LANES).astype(jnp.bfloat16)
-        written(group).start()
-
         @pl.when(turn == 0)
         def _():
             @pl.loop(1, count)
@@ -525,6 +523,17 @@
         send(here, along(here, i))
     send(here, across)
     send(here, mate)
+    @pl.loop(0, groups)
+    def _(group):
+        blocks = rows // HALO
+        wide = jnp.concatenate([ov[group, pl.ds(b * LANES, LANES), :] for b in range(blocks)], axis=1)
+        moved = jnp.dot(back, wide, preferred_element_type=jnp.float32).astype(jnp.bfloat16)
+        for b in range(blocks):
+            for g in range(ROWS8):
+                lanes = pl.ds(pl.multiple_of(group * width + g * LANES, LANES), LANES)
+                ot[pl.ds(b * HALO, HALO), lanes] = moved[g * HALO:(g + 1) * HALO, b * LANES:(b + 1) * LANES]
+        written(group).start()
+
     sacc[...] = jnp.zeros_like(sacc)
     locals_[7].wait()
     score(here)
@@ -583,7 +592,7 @@
     return pl.pallas_call(
         functools.partial(fused_kernel, count, layers, rows, channels, scale, final),
         out_shape=(
-            jax.ShapeDtypeStruct((groups, rows * ROWS8, LANES), b16),
+            jax.ShapeDtypeStruct((rows, channels), b16),
             jax.ShapeDtypeStruct((train.shape[0], LANES), f32),
         ),
         in_specs=[anywhere] * 8,
@@ -601,6 +610,7 @@
             pltpu.VMEM((rows + HALO, ROWS8, LANES), f32),
             pltpu.VMEM((layers * 5, ROWS8, LANES), f32),
             pltpu.VMEM((groups, rows * ROWS8, LANES), b16),
+            pltpu.VMEM((rows, channels), b16),
             pltpu.VMEM((count, len(PAIRS), lines, LANES), b16),
             pltpu.VMEM((count, len(PAIRS), lines, LANES), b16),
             pltpu.VMEM((count, layers * 5, lines, LANES), b16),
@@ -619,70 +629,52 @@
     )(owner_map, acts, cots, weights, bias, basis.reshape(25, tall, LANES), vals.reshape(5, tall, LANES), train)
 
 
-def finish_kernel(rows, a_hbm, v_hbm, i_hbm, out_hbm, s_hbm, av, ov, v_ref, i_ref, s_ref, load, store):
-    back = token_permutation(True)
-    blocks = rows // HALO
-    groups = a_hbm.shape[0]
-    width = ROWS8 * LANES
-
-    def read(i):
-        return pltpu.make_async_copy(a_hbm.at[i], av.at[i], load.at[i])
-
-    def write(i):
-        lanes = pl.ds(i * width, width)
-        return pltpu.make_async_copy(ov.at[:, lanes], out_hbm.at[:, lanes], store.at[i])
-
-    for i in range(groups):
-        read(i).start()
-    small = [pltpu.make_async_copy(v_hbm, v_ref, load.at[groups]),
-             pltpu.make_async_copy(i_hbm, i_ref, load.at[groups + 1])]
-    picked = pltpu.make_async_copy(s_ref, s_hbm, store.at[groups])
-    for copy in small:
+def finish_kernel(pieces, a_hbm, v_hbm, i_hbm, out_hbm, s_hbm, held, v_ref, i_ref, s_ref, load, store, small):
+    width = a_hbm.shape[0] // pieces
+    slabs = [pl.ds(i * width, width) for i in range(pieces)]
+    reads = [pltpu.make_async_copy(a_hbm.at[slab, :], held.at[slab, :], load.at[i]) for i, slab in enumerate(slabs)]
+    writes = [pltpu.make_async_copy(held.at[slab, :], out_hbm.at[slab, :], store.at[i])
+              for i, slab in enumerate(slabs)]
+    loads = [pltpu.make_async_copy(v_hbm, v_ref, small.at[0]), pltpu.make_async_copy(i_hbm, i_ref, small.at[1])]
+    for copy in reads + loads:
         copy.start()
+    for copy, onward in zip(reads, writes):
+        copy.wait()
+        onward.start()
+    for copy in loads:
+        copy.wait()
     examples = v_ref.shape[0]
     picks = i_ref.shape[1]
-    for i in range(groups):
-        read(i).wait()
-        wide = jnp.concatenate([av[i, pl.ds(b * LANES, LANES), :] for b in range(blocks)], axis=1)
-        moved = jnp.dot(back, wide, preferred_element_type=jnp.float32).astype(jnp.bfloat16)
-        for b in range(blocks):
-            for g in range(ROWS8):
-                ov[pl.ds(b * HALO, HALO), pl.ds(i * width + g * LANES, LANES)] = (
-                    moved[g * HALO:(g + 1) * HALO, b * LANES:(b + 1) * LANES])
-        write(i).start()
-        if i == 0:
-            for copy in small:
-                copy.wait()
-            local = i_ref[...] - lax.axis_index("dp") * examples
-            chosen = jnp.broadcast_to(local, (examples, picks)) == lax.broadcasted_iota(jnp.int32, (examples, picks), 0)
-            s_ref[...] = jnp.sum(jnp.where(chosen, v_ref[:, :picks], 0.0), axis=0, keepdims=True)
-            picked.start()
-    for i in range(groups):
-        write(i).wait()
+    local = i_ref[...] - lax.axis_index("dp") * examples
+    chosen = jnp.broadcast_to(local, (examples, picks)) == lax.broadcasted_iota(jnp.int32, (examples, picks), 0)
+    s_ref[...] = jnp.sum(jnp.where(chosen, v_ref[:, :picks], 0.0), axis=0, keepdims=True)
+    picked = pltpu.make_async_copy(s_ref, s_hbm, small.at[2])
+    picked.start()
+    for copy in writes:
+        copy.wait()
     picked.wait()
 
 
-def finish(moved, values, batch_index, rows):
-    groups = moved.shape[0]
+def finish(moved, values, batch_index):
     picks = batch_index.shape[0]
-    channels = groups * ROWS8 * LANES
+    pieces = 8
     anywhere = pl.BlockSpec(memory_space=pltpu.HBM)
     return pl.pallas_call(
-        functools.partial(finish_kernel, rows),
+        functools.partial(finish_kernel, pieces),
         out_shape=(
-            jax.ShapeDtypeStruct((rows, channels), jnp.bfloat16),
+            jax.ShapeDtypeStruct(moved.shape, moved.dtype),
             jax.ShapeDtypeStruct((1, picks), jnp.float32),
         ),
         in_specs=[anywhere] * 3,
         out_specs=(anywhere, anywhere),
         scratch_shapes=[
             pltpu.VMEM(moved.shape, moved.dtype),
-            pltpu.VMEM((rows, channels), moved.dtype),
             pltpu.VMEM(values.shape, values.dtype),
             pltpu.VMEM((1, picks), batch_index.dtype),
             pltpu.VMEM((1, picks), jnp.float32),
-            pltpu.SemaphoreType.DMA((groups + 2,)),
-            pltpu.SemaphoreType.DMA((groups + 1,)),
+            pltpu.SemaphoreType.DMA((pieces,)),
+            pltpu.SemaphoreType.DMA((pieces,)),
+            pltpu.SemaphoreType.DMA((3,)),
         ],
         compiler_params=pltpu.CompilerParams(vmem_limit_bytes=63 << 20),
     )(moved, values, batch_index.reshape(1, picks))
@@ -724,7 +716,7 @@
             rows % HALO == 0 and batch_index.shape[0] <= LANES):
         moved, values = fused(query_acts, cotangent, conv_weight, conv_bias, owner_map, basis_store[0],
                                 lambda_store[0], train_grads.transpose(0, 2, 1, 3), norm_scale, final)
-        adjoint, scores = finish(moved, values, batch_index, rows)
+        adjoint, scores = finish(moved, values, batch_index)
         return (adjoint, scores.reshape(-1))
     else:
         adjoint, everyone = precondition_apart(query_acts, cotangent, conv_weight, conv_bias, owner_map,

time: 57.5 us -> 51.6 us (0.90)
  the two profiles are of different devices: /device:TPU:11 before, /device:TPU:1 now
where the time goes in v4:
time: 51.6 us; the launch traced here: 51.5 us
  Pallas kernels  50.8 us (98%)
  between operations  0.64 us (1%)
    pallas_call x1, Pallas kernels, fused(): pl.pallas_call(functools.partial(fused_kernel, count, layers, rows, chann...  48.4 us
    pallas_call x1, Pallas kernels, finish(): pl.pallas_call(functools.partial(finish_kernel, pieces), out_shape=(jax.S...  2.42 us

profile of v4, /device:TPU:1, one launch (start us, length us, event | category | flops | bytes accessed | tf_op | source)
XLA Modules:
  0.0 51.5 jit_solution(11568424442971562938)
XLA Ops:
  0.6 48.4 %shard_map.104 = (bf16[128,8192]{1,0:T(8,128)(2,1)}, f32[8,128]{1,0:T(8,128)}) custom-call(s32[4]{0:T(128)} %o_hbm.1, bf16[128,8192]{1,0:T(8,128)(2,1)} %x_hbm.1, bf16[128,8192]{1,0:T(8,128)(2,1)} %c_hbm.1, f32[4,4,8192]{2,1,0:T(4,128)} %w_hbm.1, f32[4,8192]{1,0:T(4,128)} %b_hbm.1, f32[25,64,128]{2,1,0:T(8,128)} %bitcast.6, f32[5,64,128]{2,1,0:T(8,128)} %bitcast.7, ...), custom_call_target="tpu_custom_call" | custom-call | tf_op jit(solution)/shard_map/pallas_call | solution.py:592
  49.1 2.4 %shard_map.105 = (bf16[128,8192]{1,0:T(8,128)(2,1)}, f32[1,16]{1,0:T(1,128)}) custom-call(bf16[128,8192]{1,0:T(8,128)(2,1)} %get-tuple-element.6.a_hbm, f32[8,128]{1,0:T(8,128)} %get-tuple-element.7.v_hbm, s32[1,16]{1,0:T(1,128)} %bitcast.8), custom_call_target="tpu_custom_call" | custom-call | tf_op jit(solution)/shard_map/pallas_call | solution.py:662

commit v5 on v4

--- a/solution.py
+++ b/solution.py
@@ -247,7 +247,7 @@
     return values[0]
 
 
-def backward_layer(layer, layers, rows, step, tile, x_all, s_all, a_all, w_all, g_all):
+def backward_layer(layer, layers, rows, step, tile, x_all, s_all, a_all, w_all, g_all, dv_all):
     taps = [w_all[layer * TAPS + k, tile, :] * 0.5 for k in range(TAPS)]
 
     def grads(first, n):
@@ -267,11 +267,21 @@
         first = j * step
         dv = list(carry[:3]) + grads(first + 3, step)
         part = sums(first, dv, step)
-        back(first, dv, step)
+        if layer:
+            back(first, dv, step)
+        else:
+            keep_grads(first + 3, dv[3:])
         return tuple(dv[step:step + 3]) + tuple(a + b for a, b in zip(carry[3:], part))
 
+    def keep_grads(first, dv):
+        for i, value in enumerate(dv):
+            dv_all[first + i] = value
+
     zero = jnp.zeros((ROWS8, LANES), jnp.float32)
-    carry = lax.fori_loop(0, rows // step, body, tuple(grads(0, 3)) + (zero,) * (TAPS + 1))
+    early = grads(0, 3)
+    if not layer:
+        keep_grads(0, early)
+    carry = lax.fori_loop(0, rows // step, body, tuple(early) + (zero,) * (TAPS + 1))
     for k in range(TAPS + 1):
         g_all[layer * 5 + k] = 0.5 * carry[3 + k]
     extra = 3 * layer
@@ -281,9 +291,9 @@
 
 
 def fused_kernel(count, layers, rows, channels, scale, final, o_hbm, x_hbm, c_hbm, w_hbm, b_hbm, q_hbm, l_hbm, t_hbm,
-                 out_hbm, p_ref, xh, ch, wv, bv, qv, lv, w_all, x_all, s_all, a_all, g_all, ov, ot,
-                 ms, got_m, gs, got_g, part, full_p, tv, sacc, owner_ref,
-                 load, store, send_h, recv_h, send_m, recv_m, send_g, recv_g, send_p, recv_p):
+                 out_hbm, p_ref, xh, ch, wv, bv, qv, lv, w_all, x_all, s_all, a_all, g_all, dv_all, ot,
+                 ms, got_m, gs, gm, fs, got_g, part, full_p, tv, sacc, owner_ref,
+                 load, store, send_h, recv_h, send_m, recv_m, send_x, recv_x, send_g, recv_g, send_p, recv_p):
     here = lax.axis_index("dp")
     width = ROWS8 * LANES
     groups = channels // width
@@ -399,9 +409,15 @@
             [ref[pl.ds(at, HALO), pl.ds(pl.multiple_of(base + g * LANES, LANES), LANES)] for g in range(ROWS8)],
             axis=0)
 
-    def give(group, h):
-        owner = group * per + h
-        return remote(gs.at[owner], got_g.at[here], send_g.at[owner], recv_g.at[here], owner)
+    core, chip = lax.rem(here, 2), lax.div(here, 2)
+    mate = here + 1 - 2 * core
+
+    def to_mate(turn):
+        return remote(gs.at[group_at(here, turn) * 2 + 1 - core], gm.at[turn], send_x.at[turn], recv_x.at[turn], mate)
+
+    def to_owner(turn):
+        return remote(fs.at[turn], got_g.at[chip], send_g.at[turn], recv_g.at[chip],
+                      group_at(here, turn) * 2 + core)
 
     def written(group):
         return pltpu.make_async_copy(ot.at[:, lanes_of(group)], out_hbm.at[:, lanes_of(group)], store.at[group])
@@ -432,42 +448,49 @@
                 target[pl.ds(b * HALO, HALO)] = moved[:, b * LANES:(b + 1) * LANES].reshape(HALO, ROWS8, LANES)
 
         arrange(xh, x_all.at[0], rows // HALO + 2)
-        arrange(ch, a_all, rows // HALO + 1)
+        arrange(ch, a_all.at[group], rows // HALO + 1)
 
         for layer in range(layers):
             forward_layer(layer, layers, rows, (rows + 3 * layers) // 2, tile, x_all, s_all, w_all, keep)
+        @pl.when(turn > 0)
+        def _():
+            before = turn - 1
+            to_mate(before).wait_recv()
+            fs[before] = (gs[group_at(here, before) * 2 + core].astype(jnp.float32)
+                          + gm[before].astype(jnp.float32)).astype(jnp.bfloat16)
+            to_owner(before).start()
+
         for layer in reversed(range(layers)):
-            backward_layer(layer, layers, rows, 16, tile, x_all, s_all, a_all, w_all, g_all)
+            backward_layer(layer, layers, rows, 16, tile, x_all, s_all, a_all.at[group], w_all, g_all,
+                           dv_all.at[group])
 
         for h in range(per):
             for term in range(layers * 5):
                 gs[group * per + h, term] = g_all[term, h * lines:(h + 1) * lines].astype(jnp.bfloat16)
 
-        for h in range(per):
-            @pl.when(group * per + h != here)
+        to_mate(turn).start()
+
+        for part in range(4):
+            @pl.when(turn * 4 + part + 1 < count)
             def _():
-                give(group, h).start()
-
-        ov[group] = a_all[pl.ds(0, rows)].reshape(rows * ROWS8, LANES).astype(jnp.bfloat16)
-        @pl.when(turn == 0)
-        def _():
-            @pl.loop(1, count)
-            def _(step):
-                send_rows(step).start()
+                send_rows(turn * 4 + part + 1).start()
 
     @pl.loop(1, count)
     def _(step):
         send_rows(step).wait()
 
-    @pl.loop(1, count)
+    last = groups - 1
+    to_mate(last).wait_recv()
+
+    @pl.loop(1, groups)
     def _(step):
-        source = lax.rem(here + step, count)
-        remote(gs.at[source], got_g.at[source], send_g.at[source], recv_g.at[source], source).wait()
+        source = lax.rem(chip + step, groups)
+        remote(fs.at[0], got_g.at[source], send_g.at[0], recv_g.at[source], source * 2 + core).wait_recv()
 
     locals_[6].wait()
-    total = gs[here].astype(jnp.float32)
-    for step in range(1, count):
-        total = total + got_g[lax.rem(here + step, count)].astype(jnp.float32)
+    total = gs[here].astype(jnp.float32) + gm[last].astype(jnp.float32)
+    for step in range(1, groups):
+        total = total + got_g[lax.rem(chip + step, groups)].astype(jnp.float32)
     total = total * scale
     order = {pair: i for i, pair in enumerate(PAIRS)}
     for layer in range(layers):
@@ -481,8 +504,7 @@
             for r in range(lines):
                 part[j, pl.ds(layer, 1), r * LANES:(r + 1) * LANES] = value[r:r + 1]
 
-    core, side, depth = lax.rem(here, 2), lax.rem(lax.div(here, 2), 2), count // 4
-    mate = here + 1 - 2 * core
+    side, depth = lax.rem(lax.div(here, 2), 2), count // 4
     across = here + 2 - 4 * side
 
     def along(device, i):
@@ -523,17 +545,38 @@
         send(here, along(here, i))
     send(here, across)
     send(here, mate)
-    @pl.loop(0, groups)
-    def _(group):
+    def put_back(group):
         blocks = rows // HALO
-        wide = jnp.concatenate([ov[group, pl.ds(b * LANES, LANES), :] for b in range(blocks)], axis=1)
-        moved = jnp.dot(back, wide, preferred_element_type=jnp.float32).astype(jnp.bfloat16)
+        tile = pl.ds(pl.multiple_of(group * ROWS8, ROWS8), ROWS8)
+        taps = [w_all[k, tile, :] * 0.5 for k in range(TAPS)]
+        pieces = []
+        for b in range(blocks):
+            dv = [dv_all[group, b * HALO + i] for i in range(HALO + TAPS - 1)]
+            final_adjoint = [
+                a_all[group, b * HALO + i]
+                + ((taps[0] * dv[i] + taps[1] * dv[i + 1]) + (taps[2] * dv[i + 2] + taps[3] * dv[i + 3]))
+                for i in range(HALO)
+            ]
+            pieces.append(jnp.concatenate(final_adjoint, axis=0).astype(jnp.bfloat16))
+        moved = jnp.dot(back, jnp.concatenate(pieces, axis=1), preferred_element_type=jnp.float32)
+        moved = moved.astype(jnp.bfloat16)
         for b in range(blocks):
             for g in range(ROWS8):
                 lanes = pl.ds(pl.multiple_of(group * width + g * LANES, LANES), LANES)
                 ot[pl.ds(b * HALO, HALO), lanes] = moved[g * HALO:(g + 1) * HALO, b * LANES:(b + 1) * LANES]
         written(group).start()
 
+        @pl.when(here < count - 1)
+        def _():
+            halo(0, group, here + 1).wait_send()
+
+        @pl.when(here > 0)
+        def _():
+            halo(1, group, here - 1).wait_send()
+            halo(2, group, here - 1).wait_send()
+
+    split = groups
+    pl.loop(0, split)(put_back)
     sacc[...] = jnp.zeros_like(sacc)
     locals_[7].wait()
     score(here)
@@ -543,6 +586,7 @@
         send(along(here, i), mate)
     await_part(across)
     send(across, mate)
+    pl.loop(split, groups)(put_back)
     for i in range(1, depth):
         score(along(here, i))
     for i in range(1, depth):
@@ -563,17 +607,15 @@
     def _(i):
         written(i).wait()
 
-        @pl.when(here < count - 1)
-        def _():
-            halo(0, i, here + 1).wait_send()
-
-        @pl.when(here > 0)
-        def _():
-            halo(1, i, here - 1).wait_send()
-            halo(2, i, here - 1).wait_send()
-
     for copy in sends:
         copy.wait_send()
+
+    @pl.loop(0, last)
+    def _(turn):
+        to_mate(turn).wait_send()
+        to_owner(turn).wait_send()
+
+    to_mate(last).wait_send()
 
 
 def fused(acts, cots, weights, bias, owner_map, basis, vals, train, scale, final):
@@ -607,14 +649,16 @@
             pltpu.VMEM((layers * 5, tall, LANES), f32),
             pltpu.VMEM((layers, held, ROWS8, LANES), f32),
             pltpu.VMEM((layers, held, ROWS8, LANES), f32),
-            pltpu.VMEM((rows + HALO, ROWS8, LANES), f32),
+            pltpu.VMEM((groups, rows + HALO, ROWS8, LANES), f32),
             pltpu.VMEM((layers * 5, ROWS8, LANES), f32),
-            pltpu.VMEM((groups, rows * ROWS8, LANES), b16),
+            pltpu.VMEM((groups, rows + ROWS8, ROWS8, LANES), f32),
             pltpu.VMEM((rows, channels), b16),
             pltpu.VMEM((count, len(PAIRS), lines, LANES), b16),
             pltpu.VMEM((count, len(PAIRS), lines, LANES), b16),
             pltpu.VMEM((count, layers * 5, lines, LANES), b16),
-            pltpu.VMEM((count, layers * 5, lines, LANES), b16),
+            pltpu.VMEM((groups, layers * 5, lines, LANES), b16),
+            pltpu.VMEM((groups, layers * 5, lines, LANES), b16),
+            pltpu.VMEM((groups, layers * 5, lines, LANES), b16),
             pltpu.VMEM((5, layers, share), f32),
             pltpu.VMEM((5, layers, channels), f32),
             pltpu.VMEM(train.shape, b16),
@@ -622,7 +666,8 @@
             pltpu.SMEM(owner_map.shape, owner_map.dtype),
             dma((8,)), dma((groups,)),
             dma((3, groups)), dma((3, groups)),
-            dma((count,)), dma((count,)), dma((count,)), dma((count,)), dma((count,)), dma((count,)),
+            dma((count,)), dma((count,)), dma((groups,)), dma((groups,)), dma((groups,)), dma((groups,)),
+            dma((count,)), dma((count,)),
         ],
         compiler_params=pltpu.CompilerParams(
             collective_id=0, has_side_effects=True, vmem_limit_bytes=63 << 20),
@@ -712,7 +757,7 @@
     lines = channels // (LANES * count)
     examples = train_grads.shape[0]
     final = 1.0 / math.sqrt(5 * layers * channels)
-    if lines in (4, 8) and count % 4 == 0 and channels == lines * LANES * count and (
+    if lines == 4 and count % 4 == 0 and channels == lines * LANES * count and (
             rows % HALO == 0 and batch_index.shape[0] <= LANES):
         moved, values = fused(query_acts, cotangent, conv_weight, conv_bias, owner_map, basis_store[0],
                                 lambda_store[0], train_grads.transpose(0, 2, 1, 3), norm_scale, final)

time: 51.6 us -> 48.4 us (0.938)
  the two profiles are of different devices: /device:TPU:1 before, /device:TPU:11 now
where the time goes in v5:
time: 48.4 us; the launch traced here: 47.8 us
  Pallas kernels  47.1 us (97%)
  between operations  0.64 us (1%)
    pallas_call x1, Pallas kernels, fused(): pl.pallas_call(functools.partial(fused_kernel, count, layers, rows, chann...  44.7 us
    pallas_call x1, Pallas kernels, finish(): pl.pallas_call(functools.partial(finish_kernel, pieces), out_shape=(jax.S...  2.42 us

profile of v5, /device:TPU:11, one launch (start us, length us, event | category | flops | bytes accessed | tf_op | source)
XLA Modules:
  0.0 47.8 jit_solution(17423053710849242859)
XLA Ops:
  0.6 44.7 %shard_map.104 = (bf16[128,8192]{1,0:T(8,128)(2,1)}, f32[8,128]{1,0:T(8,128)}) custom-call(s32[4]{0:T(128)} %o_hbm.1, bf16[128,8192]{1,0:T(8,128)(2,1)} %x_hbm.1, bf16[128,8192]{1,0:T(8,128)(2,1)} %c_hbm.1, f32[4,4,8192]{2,1,0:T(4,128)} %w_hbm.1, f32[4,8192]{1,0:T(4,128)} %b_hbm.1, f32[25,64,128]{2,1,0:T(8,128)} %bitcast.6, f32[5,64,128]{2,1,0:T(8,128)} %bitcast.7, ...), custom_call_target="tpu_custom_call" | custom-call | tf_op jit(solution)/shard_map/pallas_call | solution.py:634
  45.4 2.4 %shard_map.105 = (bf16[128,8192]{1,0:T(8,128)(2,1)}, f32[1,16]{1,0:T(1,128)}) custom-call(bf16[128,8192]{1,0:T(8,128)(2,1)} %get-tuple-element.6.a_hbm, f32[8,128]{1,0:T(8,128)} %get-tuple-element.7.v_hbm, s32[1,16]{1,0:T(1,128)} %bitcast.8), custom_call_target="tpu_custom_call" | custom-call | tf_op jit(solution)/shard_map/pallas_call | solution.py:707

commit v6 on v5

--- a/solution.py
+++ b/solution.py
@@ -461,7 +461,7 @@
             to_owner(before).start()
 
         for layer in reversed(range(layers)):
-            backward_layer(layer, layers, rows, 16, tile, x_all, s_all, a_all.at[group], w_all, g_all,
+            backward_layer(layer, layers, rows, 32, tile, x_all, s_all, a_all.at[group], w_all, g_all,
                            dv_all.at[group])
 
         for h in range(per):

time: 48.4 us -> 48.3 us (level)
  no operation moved by 1% of the time
where the time goes in v6:
time: 48.3 us; the launch traced here: 47.6 us
  Pallas kernels  46.9 us (97%)
  between operations  0.64 us (1%)
    pallas_call x1, Pallas kernels, fused(): pl.pallas_call(functools.partial(fused_kernel, count, layers, rows, chann...  44.5 us
    pallas_call x1, Pallas kernels, finish(): pl.pallas_call(functools.partial(finish_kernel, pieces), out_shape=(jax.S...  2.42 us

profile of v6, /device:TPU:11, one launch (start us, length us, event | category | flops | bytes accessed | tf_op | source)
XLA Modules:
  0.0 47.6 jit_solution(17664158884814885368)
XLA Ops:
  0.6 44.5 %shard_map.104 = (bf16[128,8192]{1,0:T(8,128)(2,1)}, f32[8,128]{1,0:T(8,128)}) custom-call(s32[4]{0:T(128)} %o_hbm.1, bf16[128,8192]{1,0:T(8,128)(2,1)} %x_hbm.1, bf16[128,8192]{1,0:T(8,128)(2,1)} %c_hbm.1, f32[4,4,8192]{2,1,0:T(4,128)} %w_hbm.1, f32[4,8192]{1,0:T(4,128)} %b_hbm.1, f32[25,64,128]{2,1,0:T(8,128)} %bitcast.6, f32[5,64,128]{2,1,0:T(8,128)} %bitcast.7, ...), custom_call_target="tpu_custom_call" | custom-call | tf_op jit(solution)/shard_map/pallas_call | solution.py:634
  45.2 2.4 %shard_map.105 = (bf16[128,8192]{1,0:T(8,128)(2,1)}, f32[1,16]{1,0:T(1,128)}) custom-call(bf16[128,8192]{1,0:T(8,128)(2,1)} %get-tuple-element.6.a_hbm, f32[8,128]{1,0:T(8,128)} %get-tuple-element.7.v_hbm, s32[1,16]{1,0:T(1,128)} %bitcast.8), custom_call_target="tpu_custom_call" | custom-call | tf_op jit(solution)/shard_map/pallas_call | solution.py:707
